TPU v7x, 512 devices: a whole 4x8x8 slice. The times are simulated.
512 devices in a mesh: expert: 32 (over y, z_hi, core), tensor: 4 (over x), dp: 4 (over z_lo).
Axes of the slice: x: 4, y: 8, z: 8 (z_hi: 2, z_lo: 4; z = z_hi * 4 + z_lo), core: 2. Of those that a mesh axis runs over, the one named last changes fastest.
Arguments:
- tokens: bfloat16 [16384, 4096], P(('expert', 'dp'), 'tensor'), may hold values from -6 to 6
- routes: int32 [16384, 2], P(('expert', 'dp')), may hold values from 0 to 31, all different within a row; in each aligned block of 128 rows (0 to 127, 128 to 255, ...) at most 10 rows name the same one
- gate_prob: float32 [16384, 2], P(('expert', 'dp')), may hold values from 0.05 to 1
- token_count: int32 [128], P(('expert', 'dp')), may hold values from 1 to 128, 12288 in all
- gate_weight: bfloat16 [32, 4096, 1536], P(None, ('expert', 'dp'), 'tensor'), may hold values from -0.09375 to 0.09375
- up_weight: bfloat16 [32, 4096, 1536], P(None, ('expert', 'dp'), 'tensor'), may hold values from -0.09375 to 0.09375
- down_weight: bfloat16 [32, 4096, 1536], P(None, ('expert', 'dp'), 'tensor'), may hold values from -0.15625 to 0.15625
Outputs:
- mixed: bfloat16 [16384, 4096], P(('expert', 'dp'), 'tensor')
Inputs may be any that keep to these rules, and one draw needn't show every extreme that they name: `routes`: each row names 2 different experts; among the rows of one group (aligned blocks of 128 rows) no expert is named by more than 10 rows. `token_count`: rows of a group at or past its count are padding.
All inputs are finite; a program needn't handle non-finite values.
Results may differ from a plain program's by a relative error of at most 0.012.
Values may be sent and summed in bfloat16 or wider, within the bound.
A program may use at most 64 MiB of HBM per device.

v0:
```python
import jax
import jax.numpy as jnp
from jax import lax
from jax.sharding import PartitionSpec as P


def shards(tokens, routes, gate_prob, token_count, gate_weight, up_weight, down_weight):
    experts = gate_weight.shape[0]
    stored_rows = gate_weight.shape[1]
    hidden_share = gate_weight.shape[2]
    tok_rows, top_slots = routes.shape
    capacity = min(tok_rows, tok_rows * top_slots * 5 // (4 * experts))
    expert_count = lax.axis_size("expert")
    replica_count = lax.axis_size("dp")
    model_width = stored_rows * expert_count * replica_count
    arrived_rows = (
        lax.all_to_all(gate_weight, "expert", split_axis=0, concat_axis=1, tiled=True),
        lax.all_to_all(up_weight, "expert", split_axis=0, concat_axis=1, tiled=True),
        lax.all_to_all(down_weight, "expert", split_axis=0, concat_axis=1, tiled=True),
    )

    def split_blocks(weight):
        return weight.reshape(1, expert_count, 1, stored_rows, hidden_share)

    assembled = (
        lax.all_gather(split_blocks(arrived_rows[0]), "dp", axis=2, tiled=True),
        lax.all_gather(split_blocks(arrived_rows[1]), "dp", axis=2, tiled=True),
        lax.all_gather(split_blocks(arrived_rows[2]), "dp", axis=2, tiled=True),
    )
    w_gate = assembled[0].reshape(model_width, hidden_share)
    w_up = assembled[1].reshape(model_width, hidden_share)
    w_down = assembled[2].reshape(model_width, hidden_share)
    positions = jnp.arange(tok_rows)
    live_rows = positions < token_count[0]
    live_pair = jnp.repeat(live_rows, top_slots)
    route_flat = routes.reshape(-1)
    expert_ids = jnp.arange(experts)
    one_hot = ((route_flat[:, None] == expert_ids[None, :]) & live_pair[:, None]).astype(jnp.int32)
    pair_rank = jnp.sum((jnp.cumsum(one_hot, axis=0) - one_hot) * one_hot, axis=1)
    slot_of_pair = jnp.where(live_pair, route_flat * capacity + pair_rank, -1)
    slot_ids = jnp.arange(experts * capacity)
    assign_pair = (slot_ids[:, None] == slot_of_pair[None, :]).astype(jnp.bfloat16)
    assign_slots = assign_pair.reshape(experts * capacity, tok_rows, top_slots)
    assign_bf16 = jnp.sum(assign_slots.astype(jnp.float32), axis=2).astype(jnp.bfloat16)
    outgoing = jnp.dot(assign_bf16, tokens, preferred_element_type=jnp.float32).astype(jnp.bfloat16)
    incoming = lax.all_to_all(
        outgoing.reshape(experts, capacity, tokens.shape[1]),
        "expert",
        split_axis=0,
        concat_axis=0,
        tiled=True,
    )
    feature_piece = lax.all_gather(incoming, "tensor", axis=2, tiled=True)
    piece_width = feature_piece.shape[2]
    flat_piece = feature_piece.reshape(-1, piece_width)
    gate_proj = jnp.dot(flat_piece, w_gate, preferred_element_type=jnp.float32)
    up_proj = jnp.dot(flat_piece, w_up, preferred_element_type=jnp.float32)
    hidden = (jax.nn.silu(gate_proj) * up_proj).astype(jnp.bfloat16)
    partial_value = lax.dot_general(
        hidden, w_down, (((1,), (1,)), ((), ())), preferred_element_type=jnp.float32
    )
    expert_out = lax.psum_scatter(
        partial_value.astype(jnp.bfloat16), "tensor", scatter_dimension=1, tiled=True
    )
    returned = lax.all_to_all(
        expert_out.reshape(experts, capacity, -1), "expert", split_axis=0, concat_axis=0, tiled=True
    )
    returned_rows = returned.reshape(experts * capacity, -1)
    picked = jnp.einsum(
        "cts,cd->std", assign_slots, returned_rows, preferred_element_type=jnp.float32
    )
    slot_weights = gate_prob.T
    mixed = jnp.sum(slot_weights[:, :, None] * picked, axis=0)
    return mixed.astype(jnp.bfloat16)


def solution(mesh):
    in_specs = (
        P(("expert", "dp"), "tensor"),
        P(("expert", "dp"), None),
        P(("expert", "dp"), None),
        P(("expert", "dp")),
        P(None, ("expert", "dp"), "tensor"),
        P(None, ("expert", "dp"), "tensor"),
        P(None, ("expert", "dp"), "tensor"),
    )
    out_specs = P(("expert", "dp"), "tensor")
    return jax.shard_map(shards, mesh=mesh, in_specs=in_specs, out_specs=out_specs, check_vma=False)
```

profile of v0, /device:TPU:1, one launch (start us, length us, event | category | flops | bytes accessed | tf_op | source)
XLA Modules:
  0.0 439.4 jit_solution(14603103869681247513)
XLA Ops:
  6.5 0.8 copy.30
  8.4 0.1 broadcast_in_dim.17
  8.6 0.6 reduce-window.6
  9.2 0.2 slice_reduce_fusion
  9.5 0.1 and.16
  10.0 0.7 add_select_fusion
  10.7 0.3 convolution_convert_fusion.1
  11.1 0.2 reshape.115
  11.3 47.6 %all_to_all.37 = bf16[32,10,1024]{2,1,0:T(8,128)(2,1)} all-to-all(bf16[32,10,1024]{2,1,0:T(8,128)(2,1)S(1)} %reshape.115), channel_id=1, replica_groups=mesh['expert'=32,'tensor'=4,'dp'=4] {'expert'}, dimensions={0} | all-to-all | bytes 1310720 | tf_op jit(solution)/shard_map/all_to_all | solution.py:46
  59.0 31.1 %all_to_all.38 = bf16[32,32,384]{2,1,0:T(8,128)(2,1)} all-to-all(bf16[32,32,384]{2,1,0:T(8,128)(2,1)S(1)} %copy-done.1), channel_id=1, replica_groups=mesh['expert'=32,'tensor'=4,'dp'=4] {'expert'}, dimensions={0} | all-to-all | bytes 1572864 | tf_op jit(solution)/shard_map/all_to_all | solution.py:17
  90.1 30.9 %all_to_all.39 = bf16[32,32,384]{2,1,0:T(8,128)(2,1)} all-to-all(bf16[32,32,384]{2,1,0:T(8,128)(2,1)S(1)} %copy-done.2), channel_id=1, replica_groups=mesh['expert'=32,'tensor'=4,'dp'=4] {'expert'}, dimensions={0} | all-to-all | bytes 1572864 | tf_op jit(solution)/shard_map/all_to_all | solution.py:18
  121.0 30.7 %all_to_all.40 = bf16[32,32,384]{2,1,0:T(8,128)(2,1)} all-to-all(bf16[32,32,384]{2,1,0:T(8,128)(2,1)S(1)} %copy-done.3), channel_id=1, replica_groups=mesh['expert'=32,'tensor'=4,'dp'=4] {'expert'}, dimensions={0} | all-to-all | bytes 1572864 | tf_op jit(solution)/shard_map/all_to_all | solution.py:19
  151.9 3.3 reshape.116
  155.2 41.5 %all-gather.10.cloned.1.call-done = bf16[32,128,384]{2,1,0:T(8,128)(2,1)} async-done(((bf16[32,32,384]{2,1,0:T(8,128)(2,1)}), bf16[32,128,384]{2,1,0:T(8,128)(2,1)}) %all-gather.10.cloned.1.call-update) | async-done | bytes 3145744 | tf_op jit(solution)/shard_map/all_gather | solution.py:26
  196.7 3.4 fusion.21
  200.1 68.5 %all-gather.12.cloned.1.call-done = bf16[32,128,384]{2,1,0:T(8,128)(2,1)} async-done(((bf16[32,32,384]{2,1,0:T(8,128)(2,1)}), bf16[32,128,384]{2,1,0:T(8,128)(2,1)}) %all-gather.12.cloned.1.call-update) | async-done | bytes 3145744 | tf_op jit(solution)/shard_map/all_gather | solution.py:27
  268.7 71.8 %all-gather.14.cloned.1.call-done = bf16[32,128,384]{2,1,0:T(8,128)(2,1)} async-done(((bf16[32,32,384]{2,1,0:T(8,128)(2,1)}), bf16[32,128,384]{2,1,0:T(8,128)(2,1)}) %all-gather.14.cloned.1.call-update) | async-done | bytes 3145744 | tf_op jit(solution)/shard_map/all_gather | solution.py:28
  340.5 7.3 %convolution_convert_fusion = bf16[320,4096]{1,0:T(8,128)(2,1)} fusion(bf16[4096,384]{1,0:T(8,128)(2,1)} %bitcast.45, bf16[320,4096]{1,0:T(8,128)(2,1)S(1)} %reshape.116, bf16[4096,384]{1,0:T(8,128)(2,1)} %bitcast.44, f32[320,384]{1,0:T(8,128)S(1)} %fusion.21), kind=kOutput, calls=%fused_computation | convolution fusion | flops 2015313920 | bytes 12025856 | tf_op jit(solution)/shard_map/dot_general | solution.py:59
  347.8 39.7 %reduce-scatter.2.cloned.1.call-done = bf16[320,1024]{1,0:T(8,128)(2,1)} async-done(((bf16[320,4096]{1,0:T(8,128)(2,1)}), bf16[320,1024]{1,0:T(8,128)(2,1)}) %reduce-scatter.2.cloned.1.call-update) | async-done | bytes 655376 | tf_op jit(solution)/shard_map/reduce_scatter | solution.py:62
  387.5 1.3 reshape.123
  388.8 42.5 %all_to_all.41 = bf16[32,10,1024]{2,1,0:T(8,128)(2,1)S(1)} all-to-all(bf16[32,10,1024]{2,1,0:T(8,128)(2,1)S(1)} %reshape.123), channel_id=1, replica_groups=mesh['expert'=32,'tensor'=4,'dp'=4] {'expert'}, dimensions={0} | all-to-all | bytes 1310720 | tf_op jit(solution)/shard_map/all_to_all | solution.py:65
  431.3 0.2 reshape.131
  431.5 0.5 fusion.1
  432.0 0.9 copy.35
  (34 shorter events, 1.2 us)
Async XLA Ops:
  6.5 4.2 copy-start
  6.5 145.3 %all-gather.8.cloned.1.call-start = ((), (), s32[]{:S(2)}) async-start(), calls=%async_computation.6 | async-start | bytes 5242880 | tf_op jit(solution)/shard_map/all_gather | solution.py:53
  8.6 50.4 %copy-start.1 = (bf16[32,32,384]{2,1,0:T(8,128)(2,1)S(1)}, bf16[32,32,384]{2,1,0:T(8,128)(2,1)}, u32[]{:S(2)}) copy-start(bf16[32,32,384]{2,1,0:T(8,128)(2,1)} %param.11) | copy-start | bytes 2359300
  11.3 78.8 %copy-start.2 = (bf16[32,32,384]{2,1,0:T(8,128)(2,1)S(1)}, bf16[32,32,384]{2,1,0:T(8,128)(2,1)}, u32[]{:S(2)}) copy-start(bf16[32,32,384]{2,1,0:T(8,128)(2,1)} %param.12) | copy-start | bytes 2359300
  58.9 62.2 %copy-start.3 = (bf16[32,32,384]{2,1,0:T(8,128)(2,1)S(1)}, bf16[32,32,384]{2,1,0:T(8,128)(2,1)}, u32[]{:S(2)}) copy-start(bf16[32,32,384]{2,1,0:T(8,128)(2,1)} %param.13) | copy-start | bytes 2359300
  58.9 137.8 %all-gather.10.cloned.1.call-start = ((), (), s32[]{:S(2)}) async-start(), calls=%async_computation.8 | async-start | bytes 3932160 | tf_op jit(solution)/shard_map/all_gather | solution.py:26
  90.0 178.6 %all-gather.12.cloned.1.call-start = ((), (), s32[]{:S(2)}) async-start(), calls=%async_computation.9 | async-start | bytes 3932160 | tf_op jit(solution)/shard_map/all_gather | solution.py:27
  121.0 219.5 %all-gather.14.cloned.1.call-start = ((), (), s32[]{:S(2)}) async-start(), calls=%async_computation.10 | async-start | bytes 3932160 | tf_op jit(solution)/shard_map/all_gather | solution.py:28
  151.8 235.7 %reduce-scatter.2.cloned.1.call-start = ((), (), s32[]{:S(2)}) async-start(), calls=%async_computation.7 | async-start | bytes 3276800 | tf_op jit(solution)/shard_map/reduce_scatter | solution.py:62
  347.8 83.7 %copy-start.4 = (f32[128,2]{0,1:T(2,128)S(1)}, f32[128,2]{0,1:T(2,128)}, u32[]{:S(2)}) copy-start(f32[128,2]{0,1:T(2,128)} %param.9) | copy-start | bytes 3076
Sparse Core Ops, SparseCore 0:
  59.0 49.7 all-gather.7
  110.9 85.8 all-gather.9
  198.8 69.7 all-gather.11
  270.6 69.7 all-gather.13
  347.9 39.5 reduce-scatter.1
where the time goes:
time: 440 us; the launch traced here: 439 us
  waiting for transfers between devices  222 us (50%)
  blocking collectives  183 us (42%)
  between operations  14 us (3%)
  matrix products  11.5 us (3%)
  local copies, waits for them, and re-layouts  7.87 us (2%)
    all_gather x1, waiting for transfers between devices, shards(): lax.all_gather(split_blocks(arrived_rows[2]), 'dp', axis=2, tiled=True)  71.8 us
    all_gather x1, waiting for transfers between devices, shards(): lax.all_gather(split_blocks(arrived_rows[1]), 'dp', axis=2, tiled=True)  68.5 us
    all_to_all x1, blocking collectives, shards(): lax.all_to_all(outgoing.reshape(experts, capacity, tokens.shape[1]), 'exp...  47.6 us
    all_to_all x1, blocking collectives, shards(): lax.all_to_all(expert_out.reshape(experts, capacity, -1), 'expert', split...  42.5 us
    all_gather x1, waiting for transfers between devices, shards(): lax.all_gather(split_blocks(arrived_rows[0]), 'dp', axis=2, tiled=True)  41.5 us
    reduce_scatter x1, waiting for transfers between devices, shards(): lax.psum_scatter(partial_value.astype(jnp.bfloat16), 'tensor', scatter_di...  39.7 us
    all_to_all x1, blocking collectives, shards(): lax.all_to_all(gate_weight, 'expert', split_axis=0, concat_axis=1, tiled=...  31.1 us
    all_to_all x1, blocking collectives, shards(): lax.all_to_all(up_weight, 'expert', split_axis=0, concat_axis=1, tiled=True)  30.9 us
  transfers between devices with their start and end apart: 5, of which 4 were waited for; matrix products, arithmetic and copies ran while one was open for 2% of the time, Pallas kernels for 0%

commit v1 on v0

v1 whole, which is shorter than its diff:
```python
import functools

import jax
import jax.numpy as jnp
from jax import lax
from jax.experimental import pallas as pl
from jax.experimental.pallas import tpu as pltpu
from jax.sharding import PartitionSpec as P

MESH = pl.DeviceIdType.MESH
BF16 = jnp.bfloat16
F32 = jnp.float32


class Place:
    def __init__(self, nx, ny, nz, nzl):
        self.nx, self.ny, self.nz, self.nzl = nx, ny, nz, nzl
        self.nzh = nz // nzl

    def here(self):
        e = lax.axis_index("expert")
        x = lax.axis_index("tensor")
        zl = lax.axis_index("dp")
        core = lax.rem(e, 2)
        zh = lax.rem(e // 2, self.nzh)
        y = e // (2 * self.nzh)
        return x, y, zh * self.nzl + zl, core

    def dev(self, x, y, z, core):
        zh = z // self.nzl
        zl = lax.rem(z, self.nzl)
        return ((y * self.nzh + zh) * 2 + core, x, zl)


def signal_all(pos, x, y, z, c, barrier, xy, zring, core):
    n = 0
    if core:
        pl.semaphore_signal(barrier, inc=1, device_id=pos.dev(x, y, z, 1 - c), device_id_type=MESH)
        n += 1
    if zring == "ring":
        for dz in (1, pos.nz - 1):
            zz = lax.rem(z + dz, pos.nz)
            pl.semaphore_signal(barrier, inc=1, device_id=pos.dev(x, y, zz, c), device_id_type=MESH)
        n += 2
    if zring == "all":

        def zbody(k, carry):
            zz = lax.rem(z + k, pos.nz)
            pl.semaphore_signal(barrier, inc=1, device_id=pos.dev(x, y, zz, c), device_id_type=MESH)
            return carry

        lax.fori_loop(1, pos.nz, zbody, 0)
        n += pos.nz - 1
    if xy:

        def body(k, carry):
            xx = lax.rem(x + lax.rem(k, pos.nx), pos.nx)
            yy = lax.rem(y + k // pos.nx, pos.ny)
            pl.semaphore_signal(barrier, inc=1, device_id=pos.dev(xx, yy, z, c), device_id_type=MESH)
            return carry

        lax.fori_loop(1, pos.nx * pos.ny, body, 0)
        n += pos.nx * pos.ny - 1
    pl.semaphore_wait(barrier, n)


def z_exchange_kernel(pos, n, refs):
    srcs, dsts = refs[:n], refs[n : 2 * n]
    send, recv, loc = refs[2 * n : 2 * n + 3]
    x, y, z, c = pos.here()
    signal_all(pos, x, y, z, c, pltpu.get_barrier_semaphore(), False, "all", False)

    def body(k, carry):
        zz = lax.rem(z + k, pos.nz)
        for i in range(n):
            pltpu.make_async_remote_copy(
                srcs[i].at[zz], dsts[i].at[z], send.at[i], recv.at[i], device_id=pos.dev(x, y, zz, c), device_id_type=MESH
            ).start()
        return carry

    lax.fori_loop(1, pos.nz, body, 0)
    for i in range(n):
        pltpu.make_async_copy(srcs[i].at[z], dsts[i].at[z], loc.at[i]).start()
    for i in range(n):
        pltpu.make_async_copy(srcs[i].at[z], dsts[i].at[z], loc.at[i]).wait()
        part = dsts[i].at[pl.ds(0, pos.nz - 1)]
        pltpu.make_async_copy(part, part, send.at[i]).wait()
        pltpu.make_async_copy(part, part, recv.at[i]).wait()


def z_exchange(pos, cid, *arrays):
    n = len(arrays)
    any_spec = pl.BlockSpec(memory_space=pl.ANY)
    return pl.pallas_call(
        lambda *refs: z_exchange_kernel(pos, n, refs),
        out_shape=[jax.ShapeDtypeStruct(a.shape, a.dtype) for a in arrays],
        in_specs=[any_spec] * n,
        out_specs=[any_spec] * n,
        scratch_shapes=[pltpu.SemaphoreType.DMA((n,)), pltpu.SemaphoreType.DMA((n,)), pltpu.SemaphoreType.DMA((n,))],
        compiler_params=pltpu.CompilerParams(collective_id=cid, has_side_effects=True),
        name="z_exchange",
    )(*arrays)


class WeightRelay:
    def __init__(self, pos, src, dst, send, recv, fsend, frecv, loc):
        self.pos, self.src, self.dst = pos, src, dst
        self.send, self.recv, self.fsend, self.frecv, self.loc = send, recv, fsend, frecv, loc
        self.width = src.shape[2]

    def slot(self, x, y, c):
        cols = pl.ds(pl.multiple_of(x * self.width, self.width), self.width)
        return self.dst.at[y, c, :, cols]

    def start_one(self, k, me):
        pos = self.pos
        x, y, z, c = me
        xx = lax.rem(x + lax.rem(k, pos.nx), pos.nx)
        yy = lax.rem(y + k // pos.nx, pos.ny)
        pltpu.make_async_remote_copy(
            self.src.at[yy * pos.nx + xx],
            self.slot(x, y, c),
            self.send,
            self.recv.at[k],
            device_id=pos.dev(xx, yy, z, c),
            device_id_type=MESH,
        ).start()

    def start_own(self, me):
        pos = self.pos
        x, y, z, c = me
        own = self.src.at[y * pos.nx + x]
        pltpu.make_async_copy(own, self.slot(x, y, c), self.loc).start()
        pltpu.make_async_remote_copy(
            own, self.slot(x, y, c), self.fsend, self.frecv, device_id=pos.dev(x, y, z, 1 - c), device_id_type=MESH
        ).start()

    def forward_one(self, k, me):
        pos = self.pos
        x, y, z, c = me
        xs = lax.rem(x - lax.rem(k, pos.nx) + pos.nx, pos.nx)
        ys = lax.rem(y - k // pos.nx + pos.ny, pos.ny)
        block = self.slot(xs, ys, c)
        pltpu.make_async_copy(block, block, self.recv.at[k]).wait()
        pltpu.make_async_remote_copy(
            block, block, self.fsend, self.frecv, device_id=pos.dev(x, y, z, 1 - c), device_id_type=MESH
        ).start()

    def finish(self, me):
        x, y, z, c = me
        own = self.src.at[y * self.pos.nx + x]
        pltpu.make_async_copy(own, self.slot(x, y, c), self.loc).wait()
        sent = self.src.at[pl.ds(0, self.pos.nx * self.pos.ny - 1)]
        pltpu.make_async_copy(sent, sent, self.send).wait()
        whole = self.dst.at[:, 0]
        pltpu.make_async_copy(whole, whole, self.fsend).wait()
        pltpu.make_async_copy(whole, whole, self.frecv).wait()


class SlotExchange:
    def __init__(self, pos, src_at, dst_at, all_but_one, send, recv, loc):
        self.pos, self.src_at, self.dst_at, self.part = pos, src_at, dst_at, all_but_one
        self.send, self.recv, self.loc = send, recv, loc

    def start_one(self, k, me):
        pos = self.pos
        x, y, z, c = me
        xx = lax.rem(x + lax.rem(k, pos.nx), pos.nx)
        yy = lax.rem(y + k // pos.nx, pos.ny)
        pltpu.make_async_remote_copy(
            self.src_at(xx, yy), self.dst_at(x, y), self.send, self.recv, device_id=pos.dev(xx, yy, z, c), device_id_type=MESH
        ).start()

    def start_own(self, me):
        x, y, z, c = me
        pltpu.make_async_copy(self.src_at(x, y), self.dst_at(x, y), self.loc).start()

    def finish(self, me):
        x, y, z, c = me
        pltpu.make_async_copy(self.src_at(x, y), self.dst_at(x, y), self.loc).wait()
        pltpu.make_async_copy(self.part, self.part, self.send).wait()
        pltpu.make_async_copy(self.part, self.part, self.recv).wait()


def tokens_and_weights(pos, cid, slots, w_gate, w_up):
    nxy = pos.nx * pos.ny
    _, rows, feat = slots.shape
    _, depth, width = w_gate.shape

    def kernel(slots_ref, wg_ref, wu_ref, x_ref, g_ref, u_ref, sends, recvs, locs, wrecv, fsend, frecv):
        me = pos.here()
        x, y, z, c = me
        signal_all(pos, x, y, z, c, pltpu.get_barrier_semaphore(), True, None, True)
        ex = SlotExchange(
            pos,
            lambda xx, yy: slots_ref.at[yy * pos.nx + xx],
            lambda xx, yy: x_ref.at[yy, :, pl.ds(pl.multiple_of(xx * feat, feat), feat)],
            slots_ref.at[pl.ds(0, nxy - 1)],
            sends.at[0],
            recvs.at[0],
            locs.at[0],
        )
        relays = [
            WeightRelay(pos, wg_ref, g_ref, sends.at[1], wrecv.at[0], fsend.at[0], frecv.at[0], locs.at[1]),
            WeightRelay(pos, wu_ref, u_ref, sends.at[2], wrecv.at[1], fsend.at[1], frecv.at[1], locs.at[2]),
        ]

        def start(k, carry):
            for r in relays:
                r.start_one(k, me)
            ex.start_one(k, me)
            return carry

        lax.fori_loop(1, nxy, start, 0)
        ex.start_own(me)
        for r in relays:
            r.start_own(me)

        def forward(k, carry):
            for r in relays:
                r.forward_one(k, me)
            return carry

        lax.fori_loop(1, nxy, forward, 0)
        ex.finish(me)
        for r in relays:
            r.finish(me)

    any_spec = pl.BlockSpec(memory_space=pl.ANY)
    w_shape = jax.ShapeDtypeStruct((pos.ny, 2, depth, pos.nx * width), BF16)
    return pl.pallas_call(
        kernel,
        out_shape=[jax.ShapeDtypeStruct((pos.ny, rows, pos.nx * feat), BF16), w_shape, w_shape],
        in_specs=[any_spec] * 3,
        out_specs=[any_spec] * 3,
        scratch_shapes=[
            pltpu.SemaphoreType.DMA((3,)),
            pltpu.SemaphoreType.DMA((1,)),
            pltpu.SemaphoreType.DMA((3,)),
            pltpu.SemaphoreType.DMA((2, nxy)),
            pltpu.SemaphoreType.DMA((2,)),
            pltpu.SemaphoreType.DMA((2,)),
        ],
        compiler_params=pltpu.CompilerParams(collective_id=cid, has_side_effects=True),
        name="tokens_and_weights",
    )(slots, w_gate, w_up)


def reduce_and_gather(pos, cid, part_gate, part_up, w_down):
    nz = pos.nz
    nxy = pos.nx * pos.ny
    _, rows, cols = part_gate.shape
    _, depth, width = w_down.shape
    subs = 2
    half = cols // subs

    def kernel(g_ref, u_ref, wd_ref, h_ref, d_ref, land, rs_send, rs_recv, ag_send, ag_recv, sems, wrecv):
        me = pos.here()
        x, y, z, c = me
        signal_all(pos, x, y, z, c, pltpu.get_barrier_semaphore(), True, "ring", True)
        relay = WeightRelay(pos, wd_ref, d_ref, sems.at[0], wrecv, sems.at[1], sems.at[2], sems.at[3])
        after, before = lax.rem(z + 1, nz), lax.rem(z + nz - 1, nz)
        target = (pos.dev(x, y, after, c), pos.dev(x, y, before, c))
        parts = (g_ref, u_ref)

        def chunk(d, s):
            return lax.rem(z - s - 1 + 2 * nz, nz) if d == 0 else lax.rem(z + s + 1, nz)

        def rs_copy(d, sub, s, src):
            return pltpu.make_async_remote_copy(
                src, land.at[d, s, sub], rs_send.at[d, sub, s], rs_recv.at[d, sub, s], device_id=target[d], device_id_type=MESH
            )

        def cut(ref, j, sub):
            return ref.at[j, :, pl.ds(sub * half, half)]

        for sub in range(subs):
            for d in range(2):
                rs_copy(d, sub, 0, cut(parts[d], chunk(d, 0), sub)).start()

        def start(k, carry):
            relay.start_one(k, me)
            return carry

        lax.fori_loop(1, nxy, start, 0)
        relay.start_own(me)

        def rs_step(s, carry):
            for sub in range(subs):
                for d in range(2):
                    slot = land.at[d, s, sub]
                    pltpu.make_async_copy(slot, slot, rs_recv.at[d, sub, s]).wait()
                    mine = parts[d][chunk(d, s + 1), :, pl.ds(sub * half, half)]
                    slot[...] = (slot[...].astype(F32) + mine.astype(F32)).astype(BF16)
                    rs_copy(d, sub, s + 1, slot).start()
            return carry

        lax.fori_loop(0, nz - 2, rs_step, 0)

        def ag_copy(d, j, s):
            block = h_ref.at[j, :, pl.ds(d * half, half)]
            return pltpu.make_async_remote_copy(
                block, block, ag_send.at[d, s], ag_recv.at[d, s], device_id=target[d], device_id_type=MESH
            )

        last = nz - 2
        for sub in range(subs):
            total = []
            for d in range(2):
                slot = land.at[d, last, sub]
                pltpu.make_async_copy(slot, slot, rs_recv.at[d, sub, last]).wait()
                mine = parts[d][z, :, pl.ds(sub * half, half)]
                total.append(slot[...].astype(F32) + mine.astype(F32))
            gate, up = total
            h_ref[z, :, pl.ds(sub * half, half)] = (gate / (1.0 + jnp.exp(-gate)) * up).astype(BF16)
            ag_copy(sub, z, 0).start()

        def ag_index(d, s):
            return lax.rem(z - s + nz, nz) if d == 0 else lax.rem(z + s, nz)

        def ag_step(s, carry):
            for d in range(2):
                j = ag_index(d, s + 1)
                block = h_ref.at[j, :, pl.ds(d * half, half)]
                pltpu.make_async_copy(block, block, ag_recv.at[d, s]).wait()

                ag_copy(d, j, s + 1).start()
            return carry

        lax.fori_loop(0, nz - 2, ag_step, 0)

        def forward(k, carry):
            relay.forward_one(k, me)
            return carry

        lax.fori_loop(1, nxy, forward, 0)
        relay.finish(me)
        for d in range(2):
            block = h_ref.at[0, :, pl.ds(d * half, half)]
            pltpu.make_async_copy(block, block, ag_recv.at[d, nz - 2]).wait()

        def drain(s, carry):
            for d in range(2):
                for sub in range(subs):
                    slot = land.at[d, s, sub]
                    pltpu.make_async_copy(slot, slot, rs_send.at[d, sub, s]).wait()
                block = h_ref.at[0, :, pl.ds(d * half, half)]
                pltpu.make_async_copy(block, block, ag_send.at[d, s]).wait()
            return carry

        lax.fori_loop(0, nz - 1, drain, 0)

    any_spec = pl.BlockSpec(memory_space=pl.ANY)
    vmem = pl.BlockSpec(memory_space=pltpu.VMEM)
    return pl.pallas_call(
        kernel,
        out_shape=[
            jax.ShapeDtypeStruct((nz, rows, cols), BF16),
            jax.ShapeDtypeStruct((pos.ny, 2, depth, pos.nx * width), BF16),
        ],
        in_specs=[vmem, vmem, any_spec],
        out_specs=[vmem, any_spec],
        scratch_shapes=[
            pltpu.VMEM((2, nz - 1, subs, rows, half), BF16),
            pltpu.SemaphoreType.DMA((2, subs, nz - 1)),
            pltpu.SemaphoreType.DMA((2, subs, nz - 1)),
            pltpu.SemaphoreType.DMA((2, nz - 1)),
            pltpu.SemaphoreType.DMA((2, nz - 1)),
            pltpu.SemaphoreType.DMA((4,)),
            pltpu.SemaphoreType.DMA((nxy,)),
        ],
        compiler_params=pltpu.CompilerParams(collective_id=cid, has_side_effects=True),
        name="reduce_and_gather",
    )(part_gate, part_up, w_down)


def slots_back(pos, cid, out):
    nxy = pos.nx * pos.ny
    _, rows, cols = out.shape
    feat = cols // pos.nx

    def kernel(o_ref, r_ref, sems):
        me = pos.here()
        x, y, z, c = me
        signal_all(pos, x, y, z, c, pltpu.get_barrier_semaphore(), True, None, False)
        ex = SlotExchange(
            pos,
            lambda xx, yy: o_ref.at[yy, :, pl.ds(pl.multiple_of(xx * feat, feat), feat)],
            lambda xx, yy: r_ref.at[yy * pos.nx + xx],
            r_ref.at[pl.ds(0, nxy - 1)],
            sems.at[0],
            sems.at[1],
            sems.at[2],
        )

        def start(k, carry):
            ex.start_one(k, me)
            return carry

        lax.fori_loop(1, nxy, start, 0)
        ex.start_own(me)
        ex.finish(me)

    any_spec = pl.BlockSpec(memory_space=pl.ANY)
    return pl.pallas_call(
        kernel,
        out_shape=jax.ShapeDtypeStruct((nxy, rows, feat), BF16),
        in_specs=[any_spec],
        out_specs=any_spec,
        scratch_shapes=[pltpu.SemaphoreType.DMA((3,))],
        compiler_params=pltpu.CompilerParams(collective_id=cid, has_side_effects=True),
        name="slots_back",
    )(out)


def shards(pos, tokens, routes, gate_prob, token_count, gate_weight, up_weight, down_weight):
    experts, depth, width = gate_weight.shape
    nx, nz, nzl = pos.nx, pos.nz, pos.nzl
    nzh = nz // nzl
    tok, feats = tokens.shape
    top = routes.shape[1]
    cap = min(tok, tok * top * 5 // (4 * experts))
    piece = feats // nz
    group_y = feats // (depth * 2 * nz)

    new = jnp.arange(feats, dtype=jnp.int32)
    zz, rest = new // piece, new % piece
    ylo, core, row = rest // (2 * depth), rest // depth % 2, rest % depth
    old = (((ylo * nzh + zz // nzl) * 2 + core) * nzl + zz % nzl) * depth + row
    shuffle = (jnp.arange(feats, dtype=jnp.int32)[:, None] == old[None, :]).astype(BF16)
    by_z = jnp.dot(tokens, shuffle, preferred_element_type=F32).astype(BF16)
    by_z = jnp.stack([by_z[:, i * piece : (i + 1) * piece] for i in range(nz)])

    x, y, z, c = pos.here()
    positions = jnp.arange(tok, dtype=jnp.int32)
    live = positions < token_count[0]
    names = routes.T
    expert_ids = jnp.arange(experts, dtype=jnp.int32)
    named = [(expert_ids[:, None] == names[s][None, :]) & live[None, :] for s in range(top)]
    either = functools.reduce(jnp.logical_or, named).astype(BF16)
    earlier = (positions[:, None] < positions[None, :]).astype(BF16)
    rank = jnp.dot(either, earlier, preferred_element_type=F32).astype(jnp.int32)
    lines = []
    for s in range(top):
        place = (expert_ids[:, None] * nz + z) * cap + rank
        lines.append(jnp.sum(jnp.where(named[s], place + 1, 0), axis=0).astype(F32) - 1.0)
    lines += [gate_prob[:, s] for s in range(top)]
    meta = jnp.concatenate([jnp.stack(lines), jnp.zeros((8 - 2 * top, tok), F32)])
    meta = jnp.broadcast_to(meta[None], (nz, 8, tok))

    raw, infos = z_exchange(pos, 1, by_z, meta)

    slots_all = experts * nz * cap
    slot_of = [infos[:, s].astype(jnp.int32).reshape(nz * tok) for s in range(top)]
    slot_ids = jnp.arange(slots_all, dtype=jnp.int32)
    pick = functools.reduce(jnp.logical_or, [slot_ids[:, None] == s[None, :] for s in slot_of]).astype(BF16)
    outgoing = jnp.dot(pick, raw.reshape(nz * tok, piece), preferred_element_type=F32).astype(BF16)

    rows_in, w_gate, w_up = tokens_and_weights(pos, 2, outgoing.reshape(experts, nz * cap, piece), gate_weight, up_weight)

    depth_all = pos.ny * 2 * depth
    ff = nx * width
    flat = rows_in.reshape(pos.ny * nz * cap, nx * piece)
    gate = jnp.dot(flat, w_gate.reshape(depth_all, ff), preferred_element_type=F32).astype(BF16)
    up = jnp.dot(flat, w_up.reshape(depth_all, ff), preferred_element_type=F32).astype(BF16)
    chunk = flat.shape[0] // nz
    hidden, w_down = reduce_and_gather(
        pos, 3, gate.reshape(nz, chunk, ff), up.reshape(nz, chunk, ff), down_weight
    )
    out = lax.dot_general(
        hidden.reshape(nz * chunk, ff),
        w_down.reshape(depth_all, ff),
        (((1,), (1,)), ((), ())),
        preferred_element_type=F32,
    ).astype(BF16)
    back = slots_back(pos, 4, out.reshape(pos.ny, nz * cap, depth_all))
    back = back.reshape(slots_all, piece)
    mixed = jnp.zeros((nz * tok, piece), F32)
    for s in range(top):
        chosen = (slot_of[s][:, None] == slot_ids[None, :]).astype(BF16)
        prob = infos[:, top + s].reshape(nz * tok)
        mixed = mixed + prob[:, None] * jnp.dot(chosen, back, preferred_element_type=F32)
    (home,) = z_exchange(pos, 5, mixed.astype(BF16).reshape(nz, tok, piece))
    merged = jnp.concatenate([home[i] for i in range(nz)], axis=1)
    unshuffle = (old[:, None] == jnp.arange(feats, dtype=jnp.int32)[None, :]).astype(BF16)
    return jnp.dot(merged, unshuffle, preferred_element_type=F32).astype(BF16)


def solution(mesh):
    nzl = mesh.shape["dp"]
    nx = mesh.shape["tensor"]
    nzh = 2
    ny = mesh.shape["expert"] // (2 * nzh)
    pos = Place(nx, ny, nzh * nzl, nzl)
    in_specs = (
        P(("expert", "dp"), "tensor"),
        P(("expert", "dp"), None),
        P(("expert", "dp"), None),
        P(("expert", "dp")),
        P(None, ("expert", "dp"), "tensor"),
        P(None, ("expert", "dp"), "tensor"),
        P(None, ("expert", "dp"), "tensor"),
    )
    out_specs = P(("expert", "dp"), "tensor")
    return jax.shard_map(
        functools.partial(shards, pos), mesh=mesh, in_specs=in_specs, out_specs=out_specs, check_vma=False
    )
```

time: 440 us -> 232 us (0.53)
  waiting for transfers between devices: 222 us -> 0 us
  Pallas kernels: 0 us -> 193 us
  blocking collectives: 183 us -> 0 us
  between operations: 14 us -> 0.87 us
  matrix products: 11.5 us -> 23.2 us
    pallas_call x0 -> x5, Pallas kernels: none -> 193 us  [the longest x1 79.3 us: reduce_and_gather(): pl.pallas_call(kernel, out_shape=[jax.ShapeDtypeStruct((nz, rows, cols),...]
    all_to_all x5 -> x0, blocking collectives: 183 us -> none  [the longest x1 47.6 us: shards(): lax.all_to_all(outgoing.reshape(experts, capacity, tokens.shape[1]), 'exp...]
    all_gather x4 -> x0, waiting for transfers between devices: 182 us -> none  [the longest x1 71.8 us: shards(): lax.all_gather(split_blocks(arrived_rows[2]), 'dp', axis=2, tiled=True)]
    reduce_scatter x1 -> x0, waiting for transfers between devices: 39.7 us -> none  [shards(): lax.psum_scatter(partial_value.astype(jnp.bfloat16), 'tensor', scatter_di...]
    dot_general x4 -> x9, matrix products: 11.5 us -> 23.2 us  [the longest x2 5.48 us: shards(): jnp.dot(chosen, back, preferred_element_type=F32)]
    unnamed x11 -> x24, local copies, waits for them, and re-layouts: 0.85 us -> 6.24 us
    reshape x4 -> x0, local copies, waits for them, and re-layouts: 5.02 us -> none  [the longest x1 3.32 us: shards(): flat_piece = feature_piece.reshape(-1, piece_width)]
  transfers between devices with their start and end apart: 5 -> 0, of which waited for: 4 -> 0; matrix products, arithmetic and copies ran while one was open for 2% -> 0% of each run, Pallas kernels for 0% -> 0%
where the time goes in v1:
time: 232 us; the launch traced here: 227 us
  Pallas kernels  193 us (83%)
  matrix products  23.2 us (10%)
  local copies, waits for them, and re-layouts  9.17 us (4%)
    pallas_call x1, Pallas kernels, reduce_and_gather(): pl.pallas_call(kernel, out_shape=[jax.ShapeDtypeStruct((nz, rows, cols),...  79.3 us
    pallas_call x1, Pallas kernels, tokens_and_weights(): pl.pallas_call(kernel, out_shape=[jax.ShapeDtypeStruct((pos.ny, rows, pos...  63 us
    pallas_call x2, Pallas kernels, z_exchange(): pl.pallas_call(lambda *refs: z_exchange_kernel(pos, n, refs), out_shape=[...  29 us
    pallas_call x1, Pallas kernels, slots_back(): pl.pallas_call(kernel, out_shape=jax.ShapeDtypeStruct((nxy, rows, feat),...  21.9 us
    unnamed x24, local copies, waits for them, and re-layouts  6.24 us
    dot_general x2, matrix products, shards(): jnp.dot(chosen, back, preferred_element_type=F32)  5.48 us

profile of v1, /device:TPU:1, one launch (start us, length us, event | category | flops | bytes accessed | tf_op | source)
XLA Modules:
  0.0 227.5 jit_solution(623020882715515743)
XLA Ops:
  0.7 0.8 slice_bitcast_fusion.11
  1.6 0.8 slice_bitcast_fusion.8
  3.1 0.8 fusion.22
  4.8 17.3 %z_exchange.2 = (bf16[8,128,128]{2,1,0:T(8,128)(2,1)}, f32[8,8,128]{2,1,0:T(8,128)}) custom-call(bf16[8,128,128]{2,1,0:T(8,128)(2,1)} %copy-done.2, f32[8,8,128]{2,1,0:T(8,128)} %broadcast_in_dim.10.refs_1_), custom_call_target="tpu_custom_call" | custom-call | tf_op jit(solution)/shard_map/z_exchange/pallas_call | solution.py:94
  22.1 0.9 fusion.61
  23.1 4.3 %fusion.11 = bf16[2560,128]{1,0:T(8,128)(2,1)} fusion(bf16[1024,128]{1,0:T(8,128)(2,1)} %bitcast.112, s32[1024]{0:T(1024)S(1)} %bitcast.103, s32[1024]{0:T(1024)S(1)} %bitcast.100), kind=kOutput, calls=%fused_computation.16 | convolution fusion | flops 679280640 | bytes 925696 | tf_op jit(solution)/shard_map/dot_general | solution.py:457
  27.3 63.0 %tokens_and_weights.1 = (bf16[8,80,512]{2,1,0:T(8,128)(2,1)}, bf16[8,2,32,1536]{3,2,1,0:T(8,128)(2,1)}, bf16[8,2,32,1536]{3,2,1,0:T(8,128)(2,1)}) custom-call(bf16[32,80,128]{2,1,0:T(8,128)(2,1)} %bitcast.97, bf16[32,32,384]{2,1,0:T(8,128)(2,1)} %wg_ref.1, bf16[32,32,384]{2,1,0:T(8,128)(2,1)} %wu_ref.1), custom_call_target="tpu_custom_call" | custom-call | tf_op jit(solution)/shard_map/tokens_and_weights/pallas_call | solution.py:231
  90.4 4.3 %convolution_convert_fusion.1 = bf16[640,1536]{1,0:T(8,128)(2,1)} fusion(bf16[640,512]{1,0:T(8,128)(2,1)} %bitcast.110, bf16[512,1536]{1,0:T(8,128)(2,1)} %bitcast.108), kind=kOutput, calls=%fused_computation.18 | convolution fusion | flops 1007616000 | bytes 4194304 | tf_op jit(solution)/shard_map/dot_general | solution.py:464
  94.6 2.5 %convolution_convert_fusion = bf16[640,1536]{1,0:T(8,128)(2,1)} fusion(bf16[640,512]{1,0:T(8,128)(2,1)S(1)} %bitcast.111, bf16[512,1536]{1,0:T(8,128)(2,1)S(1)} %bitcast.107), kind=kOutput, calls=%fused_computation.17 | convolution fusion | flops 1007616000 | bytes 4194304 | tf_op jit(solution)/shard_map/dot_general | solution.py:465
  97.1 79.3 %reduce_and_gather.1 = (bf16[8,80,1536]{2,1,0:T(8,128)(2,1)}, bf16[8,2,32,1536]{3,2,1,0:T(8,128)(2,1)}) custom-call(bf16[8,80,1536]{2,1,0:T(8,128)(2,1)} %bitcast.92, bf16[8,80,1536]{2,1,0:T(8,128)(2,1)} %bitcast.93, bf16[32,32,384]{2,1,0:T(8,128)(2,1)} %wd_ref.1), custom_call_target="tpu_custom_call" | custom-call | tf_op jit(solution)/shard_map/reduce_and_gather/pallas_call | solution.py:355
  176.5 4.0 %convolution_convert_fusion.2 = bf16[640,512]{1,0:T(8,128)(2,1)} fusion(bf16[640,1536]{1,0:T(8,128)(2,1)} %bitcast.106, bf16[512,1536]{1,0:T(8,128)(2,1)} %bitcast.109), kind=kOutput, calls=%fused_computation.21 | convolution fusion | flops 1006960640 | bytes 4194304 | tf_op jit(solution)/shard_map/dot_general | solution.py:470
  180.5 21.9 %slots_back.1 = bf16[32,80,128]{2,1,0:T(8,128)(2,1)} custom-call(bf16[8,80,512]{2,1,0:T(8,128)(2,1)} %bitcast.96), custom_call_target="tpu_custom_call" | custom-call | tf_op jit(solution)/shard_map/slots_back/pallas_call | solution.py:405
  202.5 2.9 %fusion.16 = f32[1024,128]{1,0:T(8,128)S(1)} fusion(bf16[2560,128]{1,0:T(8,128)(2,1)} %bitcast.94, s32[1024]{0:T(1024)S(1)} %bitcast.104, f32[1024]{0:T(1024)S(1)} %bitcast.102), kind=kOutput, calls=%fused_computation.22 | convolution fusion | flops 673841152 | bytes 1187840 | tf_op jit(solution)/shard_map/dot_general | solution.py:482
  205.4 2.5 %fusion.19 = bf16[1024,128]{1,0:T(8,128)(2,1)} fusion(f32[1024,128]{1,0:T(8,128)S(1)} %fusion.16, bf16[2560,128]{1,0:T(8,128)(2,1)S(1)} %bitcast.95, s32[1024]{0:T(1024)S(1)} %bitcast.101, f32[1024]{0:T(1024)S(1)} %bitcast.99), kind=kOutput, calls=%fused_computation.25 | convolution fusion | flops 674103296 | bytes 1449984 | tf_op jit(solution)/shard_map/dot_general | solution.py:482
  208.0 11.6 %z_exchange.3 = bf16[8,128,128]{2,1,0:T(8,128)(2,1)} custom-call(bf16[8,128,128]{2,1,0:T(8,128)(2,1)} %bitcast.98), custom_call_target="tpu_custom_call" | custom-call | tf_op jit(solution)/shard_map/z_exchange/pallas_call | solution.py:94
  219.6 0.8 constant_dynamic-update-slice_fusion.15
  220.4 0.8 constant_dynamic-update-slice_fusion.14
  221.2 0.8 constant_dynamic-update-slice_fusion.13
  221.9 0.8 constant_dynamic-update-slice_fusion.12
  222.7 0.8 constant_dynamic-update-slice_fusion.11
  223.5 0.8 constant_dynamic-update-slice_fusion.10
  224.2 0.8 constant_dynamic-update-slice_fusion.9
  225.0 0.8 constant_dynamic-update-slice_fusion.8
  225.8 1.7 fusion.20
  (26 shorter events, 1.7 us)
Async XLA Ops:
  0.0 3.1 %copy-start = (bf16[128,1024]{1,0:T(8,128)(2,1)S(1)}, bf16[128,1024]{1,0:T(8,128)(2,1)}, u32[]{:S(2)}) copy-start(bf16[128,1024]{1,0:T(8,128)(2,1)} %param.7) | copy-start | bytes 786436
  4.1 0.7 copy-start.2
  90.4 4.3 %copy-start.3 = (bf16[8,2,32,1536]{3,2,1,0:T(8,128)(2,1)S(1)}, bf16[8,2,32,1536]{3,2,1,0:T(8,128)(2,1)}, u32[]{:S(2)}) copy-start(bf16[8,2,32,1536]{3,2,1,0:T(8,128)(2,1)} %get-tuple-element.16) | copy-start | bytes 4718596
  90.4 4.3 %copy-start.4 = (bf16[8,80,512]{2,1,0:T(8,128)(2,1)S(1)}, bf16[8,80,512]{2,1,0:T(8,128)(2,1)}, u32[]{:S(2)}) copy-start(bf16[8,80,512]{2,1,0:T(8,128)(2,1)} %get-tuple-element.14) | copy-start | bytes 1966084
  202.5 3.0 %copy-start.1 = (bf16[32,80,128]{2,1,0:T(8,128)(2,1)S(1)}, bf16[32,80,128]{2,1,0:T(8,128)(2,1)}, u32[]{:S(2)}) copy-start(bf16[32,80,128]{2,1,0:T(8,128)(2,1)} %slots_back.1) | copy-start | bytes 1966084

commit v2 on v0

v2 whole, which is shorter than its diff:
```python
import functools

import jax
import jax.numpy as jnp
from jax import lax
from jax.experimental import pallas as pl
from jax.experimental.pallas import tpu as pltpu
from jax.sharding import PartitionSpec as P

MESH = pl.DeviceIdType.MESH
BF16 = jnp.bfloat16
F32 = jnp.float32


class Place:
    def __init__(self, nx, ny, nz, nzl):
        self.nx, self.ny, self.nz, self.nzl = nx, ny, nz, nzl
        self.nzh = nz // nzl

    def here(self):
        e = lax.axis_index("expert")
        x = lax.axis_index("tensor")
        zl = lax.axis_index("dp")
        core = lax.rem(e, 2)
        zh = lax.rem(e // 2, self.nzh)
        y = e // (2 * self.nzh)
        return x, y, zh * self.nzl + zl, core

    def dev(self, x, y, z, core):
        zh = z // self.nzl
        zl = lax.rem(z, self.nzl)
        return ((y * self.nzh + zh) * 2 + core, x, zl)


def signal_all(pos, x, y, z, c, barrier, xy, zring, core):
    n = 0
    if core:
        pl.semaphore_signal(barrier, inc=1, device_id=pos.dev(x, y, z, 1 - c), device_id_type=MESH)
        n += 1
    if zring == "ring":
        for dz in (1, pos.nz - 1):
            zz = lax.rem(z + dz, pos.nz)
            pl.semaphore_signal(barrier, inc=1, device_id=pos.dev(x, y, zz, c), device_id_type=MESH)
        n += 2
    if zring == "all":

        def zbody(k, carry):
            zz = lax.rem(z + k, pos.nz)
            pl.semaphore_signal(barrier, inc=1, device_id=pos.dev(x, y, zz, c), device_id_type=MESH)
            return carry

        lax.fori_loop(1, pos.nz, zbody, 0)
        n += pos.nz - 1
    if xy:

        def body(k, carry):
            xx = lax.rem(x + lax.rem(k, pos.nx), pos.nx)
            yy = lax.rem(y + k // pos.nx, pos.ny)
            pl.semaphore_signal(barrier, inc=1, device_id=pos.dev(xx, yy, z, c), device_id_type=MESH)
            return carry

        lax.fori_loop(1, pos.nx * pos.ny, body, 0)
        n += pos.nx * pos.ny - 1
    pl.semaphore_wait(barrier, n)


def relay_kernel(pos, dims, refs):
    nx, ny, nz = pos.nx, pos.ny, pos.nz
    nxy = nx * ny
    parts, cap8, piece, top = dims["parts"], dims["rows"], dims["piece"], dims["top"]
    depth, lane = dims["depth"], dims["lane"]
    rows = cap8
    half = nx * lane // 2
    (tok_ref, meta_ref, wg_ref, wu_ref, wd_ref, back_ref, info_ref) = refs[:7]
    (raw, out_tok, x_in, wbuf, part, land, hid, acc, out) = refs[7:16]
    (zsend, zrecv, loc, wsend, wrecv, fsend, frecv, tsend, trecv, rsend, rrecv, asend, arecv, bsem) = refs[16:]
    me = pos.here()
    x, y, z, c = me
    weights = (wg_ref, wu_ref, wd_ref)
    partner = pos.dev(x, y, z, 1 - c)

    def remote(src, dst, s, r, dev):
        return pltpu.make_async_remote_copy(src, dst, s, r, device_id=dev, device_id_type=MESH)

    def wait(ref, sem):
        pltpu.make_async_copy(ref, ref, sem).wait()

    signal_all(pos, x, y, z, c, pltpu.get_barrier_semaphore(), True, "all", True)

    def raw_send(k, carry):
        zz = lax.rem(z + k, nz)
        dev = pos.dev(x, y, zz, c)
        cols = pl.ds(pl.multiple_of(zz * piece, piece), piece)
        remote(meta_ref, info_ref.at[z], zsend.at[1], zrecv.at[1], dev).start()
        remote(tok_ref.at[:, cols], raw.at[z], zsend.at[0], zrecv.at[0], dev).start()
        return carry

    lax.fori_loop(1, nz, raw_send, 0)
    own_cols = pl.ds(pl.multiple_of(z * piece, piece), piece)
    own_raw = pltpu.make_async_copy(tok_ref.at[:, own_cols], raw.at[z], loc.at[0])
    own_meta = pltpu.make_async_copy(meta_ref, info_ref.at[z], loc.at[1])
    own_raw.start()
    own_meta.start()

    def w_src(m, w, e):
        return weights[m].at[e, :, pl.ds(w * lane, lane)]

    def w_dst(m, w, xs, ys, cs):
        return wbuf.at[w, m, ys, cs, :, pl.ds(pl.multiple_of(xs * lane, lane), lane)]

    def w_start(w, mats):
        def body(k, carry):
            xx = lax.rem(x + lax.rem(k, nx), nx)
            yy = lax.rem(y + k // nx, ny)
            dev = pos.dev(xx, yy, z, c)
            for m in mats:
                remote(w_src(m, w, yy * nx + xx), w_dst(m, w, x, y, c), wsend.at[m, w], wrecv.at[m, w], dev).start()
            return carry

        lax.fori_loop(1, nxy, body, 0)
        for m in mats:
            pltpu.make_async_copy(w_src(m, w, y * nx + x), w_dst(m, w, x, y, c), loc.at[2 + 3 * w + m]).start()

    def w_forward(w, mats):
        for m in mats:
            pltpu.make_async_copy(w_src(m, w, y * nx + x), w_dst(m, w, x, y, c), loc.at[2 + 3 * w + m]).wait()
            wait(weights[m].at[pl.ds(0, nxy - 1), :, pl.ds(w * lane, lane)], wrecv.at[m, w])
            block = wbuf.at[w, m, :, c]
            remote(block, block, fsend.at[m, w], frecv.at[m, w], partner).start()

    def w_ready(w, mats):
        for m in mats:
            wait(wbuf.at[w, m, :, 0], frecv.at[m, w])

    w_start(0, (0, 1))

    own_raw.wait()
    own_meta.wait()
    for i, ref in ((1, info_ref), (0, raw)):
        wait(ref.at[pl.ds(0, nz - 1)], zsend.at[i])
        wait(ref.at[pl.ds(0, nz - 1)], zrecv.at[i])
    count = nx * rows

    def dispatch(dy):
        yy = lax.rem(y + dy, ny)
        ids = lax.broadcasted_iota(jnp.int32, (count, raw.shape[1]), 0).astype(F32)
        base = (yy * count).astype(F32)
        picks = []
        for zz in range(nz):
            hit = None
            for s in range(top):
                same = ids == (info_ref[zz, s : s + 1, :] - base)
                hit = same if hit is None else hit | same
            picks.append(jnp.where(hit, 1.0, 0.0).astype(BF16))
        pick = jnp.concatenate(picks, axis=1)
        feats = raw[...].reshape(nz * raw.shape[1], piece)
        got = jnp.dot(pick, feats, preferred_element_type=F32).astype(BF16)
        out_tok[pl.ds(yy * nx, nx)] = got.reshape(nx, rows, piece)

    def t_dst(xs, ys):
        return x_in.at[ys, :, pl.ds(pl.multiple_of(xs * piece, piece), piece)]

    def t_send(dy, first):
        yy = lax.rem(y + dy, ny)
        for dx in range(first, nx):
            xx = lax.rem(x + dx, nx)
            remote(out_tok.at[yy * nx + xx], t_dst(x, y), tsend, trecv, pos.dev(xx, yy, z, c)).start()

    dispatch(1)

    def d_body(dy, carry):
        dispatch(dy)
        t_send(dy - 1, 0)
        return carry

    lax.fori_loop(2, ny, d_body, 0)
    dispatch(0)
    t_send(ny - 1, 0)
    w_start(1, (0, 1))
    t_send(0, 1)
    own_tok = pltpu.make_async_copy(out_tok.at[y * nx + x], t_dst(x, y), loc.at[11])
    own_tok.start()
    w_forward(0, (0, 1))

    def product(w):
        wide = nx * lane
        for m in range(2):
            right = wbuf[w, m].reshape(ny * 2 * depth, wide)

            def body(i, carry):
                left = x_in[pl.ds(i * (ny // 2), ny // 2)].reshape(ny // 2 * rows, nx * piece)
                res = jnp.dot(left, right, preferred_element_type=F32).astype(BF16)
                part[w, pl.ds(i * (ny // 2), ny // 2), :, m * wide : (m + 1) * wide] = res.reshape(ny // 2, rows, wide)
                return carry

            lax.fori_loop(0, 2, body, 0)

    step = (1, nz - 1)
    near = (pos.dev(x, y, lax.rem(z + 1, nz), c), pos.dev(x, y, lax.rem(z + nz - 1, nz), c))
    far = nz // 2
    chains = [(d, h, far if h == d else far - 1) for h in range(2) for d in range(2)]
    wide = nx * lane

    def at(d, k):
        return lax.rem(z + (k if d == 0 else -k) + 2 * nz, nz)

    def rs_send(w, d, h, i, src):
        remote(src, land.at[w, d, h, i], rsend.at[w, d, h, i], rrecv.at[w, d, h, i], near[d]).start()

    def rs_start(w):
        for d, h, n in chains:
            rs_send(w, d, h, 0, part.at[w, at(d, n), :, pl.ds(h * wide, wide)])

    def rs_mid(w, i):
        for d, h, n in chains:
            if i < n:
                slot = land.at[w, d, h, i - 1]
                wait(slot, rrecv.at[w, d, h, i - 1])
                mine = part[w, at(d, n - i), :, pl.ds(h * wide, wide)]
                slot[...] = (slot[...].astype(F32) + mine.astype(F32)).astype(BF16)
        for d, h, n in chains:
            if i < n:
                rs_send(w, d, h, i, land.at[w, d, h, i - 1])

    def ag_send(w, d, h, i, j):
        block = hid.at[w, j, :, pl.ds(h * half, half)]
        remote(block, block, asend.at[w, d, h, i], arecv.at[w, d, h, i], near[d]).start()

    def rs_final(w):
        total = []
        for h in range(2):
            t = part[w, z, :, pl.ds(h * wide, wide)].astype(F32)
            for d, hh, n in chains:
                if hh == h:
                    slot = land.at[w, d, h, n - 1]
                    wait(slot, rrecv.at[w, d, h, n - 1])
                    t = t + slot[...].astype(F32)
            total.append(t)
        gate, up = total
        hid[w, z] = (gate / (1.0 + jnp.exp(-gate)) * up).astype(BF16)

    def ag_start(w):
        for d, h, n in chains:
            ag_send(w, d, h, 0, z)

    def ag_mid(w, i):
        for d, h, n in chains:
            if i <= n:
                j = at(d, -i)
                wait(hid.at[w, j, :, pl.ds(h * half, half)], arecv.at[w, d, h, i - 1])
                if i < n:
                    ag_send(w, d, h, i, j)

    def down(w, left):
        return lax.dot_general(
            left, wbuf[w, 2].reshape(ny * 2 * depth, wide), (((1,), (1,)), ((), ())), preferred_element_type=F32
        )

    def accumulate(w):
        def body(i, carry):
            span = pl.ds(i * (nz // 2), nz // 2)
            res = down(w, hid[w, span].reshape(nz // 2 * rows, wide)).reshape(nz // 2, rows, ny * 2 * depth)
            acc[span] = res if w == 0 else acc[span] + res
            return carry

        lax.fori_loop(0, 2, body, 0)

    def o_src(xx, j):
        return out.at[j, :, pl.ds(pl.multiple_of(xx * piece, piece), piece)]

    def finish_rows(js):
        last = parts - 1
        left = jnp.concatenate([hid[last, j] for j in js], axis=0) if len(js) > 1 else hid[last, js[0]]
        res = down(last, left)
        for i, j in enumerate(js):
            out[j] = (acc[j] + res[i * rows : (i + 1) * rows]).astype(BF16)

    def send_rows(js):
        for j in js:
            for dx in range(nx):
                xx = lax.rem(x + dx, nx)
                away = remote(o_src(xx, j), back_ref.at[y * nx + x], bsem.at[0], bsem.at[1], pos.dev(xx, j, z, c))
                if dx:
                    away.start()
                else:

                    @pl.when(j != y)
                    def _():
                        away.start()

                    @pl.when(j == y)
                    def _():
                        pltpu.make_async_copy(o_src(x, y), back_ref.at[y * nx + x], bsem.at[2]).start()

    own_tok.wait()
    wait(out_tok.at[pl.ds(0, nxy - 1)], tsend)
    wait(out_tok.at[pl.ds(0, nxy - 1)], trecv)
    w_ready(0, (0, 1))
    product(0)
    rs_start(0)
    w_start(2, (0, 1))
    rs_mid(0, 1)
    w_forward(1, (0, 1))
    rs_mid(0, 2)
    w_ready(1, (0, 1))
    product(1)
    rs_start(1)
    for w in range(parts):
        w_start(w, (2,))
    rs_mid(0, 3)
    rs_mid(1, 1)
    rs_final(0)
    w_forward(2, (0, 1))
    ag_start(0)
    rs_mid(1, 2)
    w_ready(2, (0, 1))
    product(2)
    rs_start(2)
    ag_mid(0, 1)
    rs_mid(1, 3)
    rs_mid(2, 1)
    ag_mid(0, 2)
    rs_final(1)
    ag_start(1)
    rs_mid(2, 2)
    ag_mid(0, 3)
    ag_mid(1, 1)
    w_forward(0, (2,))
    rs_mid(2, 3)
    ag_mid(0, 4)
    ag_mid(1, 2)
    w_ready(0, (2,))
    accumulate(0)
    rs_final(2)
    w_forward(1, (2,))
    ag_start(2)
    ag_mid(1, 3)
    w_forward(2, (2,))
    ag_mid(1, 4)
    w_ready(1, (2,))
    w_ready(2, (2,))
    ag_mid(2, 1)
    accumulate(1)
    finish_rows([z])
    ag_mid(2, 2)
    finish_rows([at(0, 1), at(1, 1)])
    send_rows([z])
    ag_mid(2, 3)
    finish_rows([at(0, 2), at(1, 2)])
    send_rows([at(0, 1), at(1, 1)])
    ag_mid(2, 4)
    finish_rows([at(0, 3), at(1, 3)])
    send_rows([at(0, 2), at(1, 2)])
    finish_rows([at(0, 4)])
    send_rows([at(0, 3), at(1, 3), at(0, 4)])

    for m in range(3):
        for w in range(parts):
            wait(weights[m].at[pl.ds(0, nxy - 1), :, pl.ds(w * lane, lane)], wsend.at[m, w])
            wait(wbuf.at[w, m, :, 0], fsend.at[m, w])
    for w in range(parts):
        for d, h, n in chains:
            for i in range(n):
                wait(land.at[w, d, h, i], rsend.at[w, d, h, i])
                wait(hid.at[w, z, :, pl.ds(h * half, half)], asend.at[w, d, h, i])
    pltpu.make_async_copy(o_src(x, y), back_ref.at[y * nx + x], bsem.at[2]).wait()
    wait(back_ref.at[pl.ds(0, nxy - 1)], bsem.at[0])
    wait(back_ref.at[pl.ds(0, nxy - 1)], bsem.at[1])


def relay(pos, cid, by_z, meta, w_gate, w_up, w_down, cap):
    nx, ny, nz = pos.nx, pos.ny, pos.nz
    nxy = nx * ny
    _, depth, width = w_gate.shape
    tok, feats = by_z.shape
    piece = feats // nz
    lane = 128
    parts = width // lane
    rows = nz * cap
    wide = nx * lane
    dims = {"parts": parts, "rows": rows, "piece": piece, "top": 2, "depth": depth, "lane": lane}
    any_spec = pl.BlockSpec(memory_space=pl.ANY)
    vmem = pl.BlockSpec(memory_space=pltpu.VMEM)
    dma = pltpu.SemaphoreType.DMA
    return pl.pallas_call(
        lambda *refs: relay_kernel(pos, dims, refs),
        out_shape=[
            jax.ShapeDtypeStruct((nxy, rows, piece), BF16),
            jax.ShapeDtypeStruct((nz, *meta.shape), F32),
        ],
        in_specs=[vmem, vmem, any_spec, any_spec, any_spec],
        out_specs=[vmem, vmem],
        scratch_shapes=[
            pltpu.VMEM((nz, tok, piece), BF16),
            pltpu.VMEM((nxy, rows, piece), BF16),
            pltpu.VMEM((ny, rows, nx * piece), BF16),
            pltpu.VMEM((parts, 3, ny, 2, depth, wide), BF16),
            pltpu.VMEM((parts, nz, rows, 2 * wide), BF16),
            pltpu.VMEM((parts, 2, 2, nz // 2, rows, wide), BF16),
            pltpu.VMEM((parts, nz, rows, wide), BF16),
            pltpu.VMEM((nz, rows, ny * 2 * depth), F32),
            pltpu.VMEM((nz, rows, nx * piece), BF16),
            dma((2,)),
            dma((2,)),
            dma((12,)),
            dma((3, parts)),
            dma((3, parts)),
            dma((3, parts)),
            dma((3, parts)),
            dma,
            dma,
            dma((parts, 2, 2, nz // 2)),
            dma((parts, 2, 2, nz // 2)),
            dma((parts, 2, 2, nz // 2)),
            dma((parts, 2, 2, nz // 2)),
            dma((3,)),
        ],
        compiler_params=pltpu.CompilerParams(
            collective_id=cid, has_side_effects=True, vmem_limit_bytes=56 * 1024 * 1024
        ),
        name="relay",
    )(by_z, meta, w_gate, w_up, w_down)


def home_exchange(pos, cid, mixed):
    nz, tok, piece = mixed.shape

    def kernel(src, dst, sems):
        x, y, z, c = pos.here()
        signal_all(pos, x, y, z, c, pltpu.get_barrier_semaphore(), False, "all", False)
        cols = dst.at[:, pl.ds(pl.multiple_of(z * piece, piece), piece)]

        def body(k, carry):
            zz = lax.rem(z + k, nz)
            pltpu.make_async_remote_copy(
                src.at[zz], cols, sems.at[0], sems.at[1], device_id=pos.dev(x, y, zz, c), device_id_type=MESH
            ).start()
            return carry

        lax.fori_loop(1, nz, body, 0)
        own = pltpu.make_async_copy(src.at[z], cols, sems.at[2])
        own.start()
        own.wait()
        part = src.at[pl.ds(0, nz - 1)]
        pltpu.make_async_copy(part, part, sems.at[0]).wait()
        pltpu.make_async_copy(part, part, sems.at[1]).wait()

    vmem = pl.BlockSpec(memory_space=pltpu.VMEM)
    return pl.pallas_call(
        kernel,
        out_shape=jax.ShapeDtypeStruct((tok, nz * piece), mixed.dtype),
        in_specs=[vmem],
        out_specs=vmem,
        scratch_shapes=[pltpu.SemaphoreType.DMA((3,))],
        compiler_params=pltpu.CompilerParams(collective_id=cid, has_side_effects=True),
        name="home_exchange",
    )(mixed)


def shards(pos, tokens, routes, gate_prob, token_count, gate_weight, up_weight, down_weight):
    experts, depth, _ = gate_weight.shape
    nz, nzl = pos.nz, pos.nzl
    nzh = nz // nzl
    tok, feats = tokens.shape
    top = routes.shape[1]
    cap = min(tok, tok * top * 5 // (4 * experts))
    piece = feats // nz

    new = jnp.arange(feats, dtype=jnp.int32)
    zz, rest = new // piece, new % piece
    ylo, core, row = rest // (2 * depth), rest // depth % 2, rest % depth
    old = (((ylo * nzh + zz // nzl) * 2 + core) * nzl + zz % nzl) * depth + row
    shuffle = (jnp.arange(feats, dtype=jnp.int32)[:, None] == old[None, :]).astype(BF16)
    by_z = jnp.dot(tokens, shuffle, preferred_element_type=F32).astype(BF16)

    x, y, z, c = pos.here()
    positions = jnp.arange(tok, dtype=jnp.int32)
    live = positions < token_count[0]
    names = routes.T
    expert_ids = jnp.arange(experts, dtype=jnp.int32)
    named = [(expert_ids[:, None] == names[s][None, :]) & live[None, :] for s in range(top)]
    either = functools.reduce(jnp.logical_or, named).astype(BF16)
    earlier = (positions[:, None] < positions[None, :]).astype(BF16)
    rank = jnp.dot(either, earlier, preferred_element_type=F32).astype(jnp.int32)
    lines = []
    for s in range(top):
        place = (expert_ids[:, None] * nz + z) * cap + rank
        lines.append(jnp.sum(jnp.where(named[s], place + 1, 0), axis=0).astype(F32) - 1.0)
    lines += [gate_prob[:, s] for s in range(top)]
    meta = jnp.concatenate([jnp.stack(lines), jnp.zeros((8 - 2 * top, tok), F32)])

    back, infos = relay(pos, 1, by_z, meta, gate_weight, up_weight, down_weight, cap)

    slots_all = experts * nz * cap
    slot_of = [infos[:, s].astype(jnp.int32).reshape(nz * tok) for s in range(top)]
    slot_ids = jnp.arange(slots_all, dtype=jnp.int32)
    back = back.reshape(slots_all, piece)
    mixed = jnp.zeros((nz * tok, piece), F32)
    for s in range(top):
        chosen = (slot_of[s][:, None] == slot_ids[None, :]).astype(BF16)
        prob = infos[:, top + s].reshape(nz * tok)
        mixed = mixed + prob[:, None] * jnp.dot(chosen, back, preferred_element_type=F32)
    merged = home_exchange(pos, 2, mixed.astype(BF16).reshape(nz, tok, piece))
    unshuffle = (old[:, None] == jnp.arange(feats, dtype=jnp.int32)[None, :]).astype(BF16)
    return jnp.dot(merged, unshuffle, preferred_element_type=F32).astype(BF16)


def solution(mesh):
    nzl = mesh.shape["dp"]
    nx = mesh.shape["tensor"]
    nzh = 2
    ny = mesh.shape["expert"] // (2 * nzh)
    pos = Place(nx, ny, nzh * nzl, nzl)
    in_specs = (
        P(("expert", "dp"), "tensor"),
        P(("expert", "dp"), None),
        P(("expert", "dp"), None),
        P(("expert", "dp")),
        P(None, ("expert", "dp"), "tensor"),
        P(None, ("expert", "dp"), "tensor"),
        P(None, ("expert", "dp"), "tensor"),
    )
    out_specs = P(("expert", "dp"), "tensor")
    return jax.shard_map(
        functools.partial(shards, pos), mesh=mesh, in_specs=in_specs, out_specs=out_specs, check_vma=False
    )
```

time: 440 us -> 164 us (0.37)
  waiting for transfers between devices: 222 us -> 0 us
  blocking collectives: 183 us -> 0 us
  Pallas kernels: 0 us -> 150 us
  between operations: 14 us -> 0.77 us
  local copies, waits for them, and re-layouts: 7.87 us -> 2.14 us
    all_to_all x5 -> x0, blocking collectives: 183 us -> none  [the longest x1 47.6 us: shards(): lax.all_to_all(outgoing.reshape(experts, capacity, tokens.shape[1]), 'exp...]
    all_gather x4 -> x0, waiting for transfers between devices: 182 us -> none  [the longest x1 71.8 us: shards(): lax.all_gather(split_blocks(arrived_rows[2]), 'dp', axis=2, tiled=True)]
    pallas_call x0 -> x2, Pallas kernels: none -> 150 us  [the longest x1 126 us: relay(): pl.pallas_call(lambda *refs: relay_kernel(pos, dims, refs), out_shape=[ja...]
    reduce_scatter x1 -> x0, waiting for transfers between devices: 39.7 us -> none  [shards(): lax.psum_scatter(partial_value.astype(jnp.bfloat16), 'tensor', scatter_di...]
    reshape x4 -> x0, local copies, waits for them, and re-layouts: 5.02 us -> none  [the longest x1 3.32 us: shards(): flat_piece = feature_piece.reshape(-1, piece_width)]
    dot_general x4 -> x5, matrix products: 11.5 us -> 9.8 us  [the longest x2 5.48 us: shards(): jnp.dot(chosen, back, preferred_element_type=F32)]
  transfers between devices with their start and end apart: 5 -> 0, of which waited for: 4 -> 0; matrix products, arithmetic and copies ran while one was open for 2% -> 0% of each run, Pallas kernels for 0% -> 0%
where the time goes in v2:
time: 164 us; the launch traced here: 163 us
  Pallas kernels  150 us (91%)
  matrix products  9.8 us (6%)
  local copies, waits for them, and re-layouts  2.14 us (1%)
    pallas_call x1, Pallas kernels, relay(): pl.pallas_call(lambda *refs: relay_kernel(pos, dims, refs), out_shape=[ja...  126 us
    pallas_call x1, Pallas kernels, home_exchange(): pl.pallas_call(kernel, out_shape=jax.ShapeDtypeStruct((tok, nz * piece),...  23.8 us
    dot_general x2, matrix products, shards(): jnp.dot(chosen, back, preferred_element_type=F32)  5.48 us

profile of v2, /device:TPU:1, one launch (start us, length us, event | category | flops | bytes accessed | tf_op | source)
XLA Modules:
  0.0 163.4 jit_solution(3069433418869909047)
XLA Ops:
  0.0 0.0 copy-start
  0.7 0.8 slice_bitcast_fusion.3
  1.5 0.1 select_reduce_fusion
  1.6 0.8 slice_bitcast_fusion
  2.4 0.6 concatenate.3.refs_1_
  3.0 0.0 copy-done
  3.1 1.5 fusion.14.refs_0_
  4.6 126.0 %relay.1 = (bf16[32,80,128]{2,1,0:T(8,128)(2,1)}, f32[8,8,128]{2,1,0:T(8,128)}) custom-call(bf16[128,1024]{1,0:T(8,128)(2,1)} %fusion.14.refs_0_, f32[8,128]{1,0:T(8,128)} %concatenate.3.refs_1_, bf16[32,32,384]{2,1,0:T(8,128)(2,1)} %refs_2_.1, bf16[32,32,384]{2,1,0:T(8,128)(2,1)} %refs_3_.1, bf16[32,32,384]{2,1,0:T(8,128)(2,1)} %refs_4_.1), custom_call_target="tpu_custom_call" | custom-call | tf_op jit(solution)/shard_map/relay/pallas_call | solution.py:385
  130.6 0.9 fusion.53
  131.5 0.0 copy-start.1
  131.5 3.0 %fusion.8 = f32[1024,128]{1,0:T(8,128)S(1)} fusion(bf16[2560,128]{1,0:T(8,128)(2,1)} %bitcast.33, s32[1024]{0:T(1024)S(1)} %bitcast.30, f32[1024]{0:T(1024)S(1)} %bitcast.31), kind=kOutput, calls=%fused_computation.12 | convolution fusion | flops 673841152 | bytes 1187840 | tf_op jit(solution)/shard_map/dot_general | solution.py:502
  134.5 0.0 copy-done.1
  134.5 2.5 %fusion.11 = bf16[1024,128]{1,0:T(8,128)(2,1)} fusion(f32[1024,128]{1,0:T(8,128)S(1)} %fusion.8, bf16[2560,128]{1,0:T(8,128)(2,1)S(1)} %bitcast.34, s32[1024]{0:T(1024)S(1)} %bitcast.29, f32[1024]{0:T(1024)S(1)} %bitcast.28), kind=kOutput, calls=%fused_computation.15 | convolution fusion | flops 674103296 | bytes 1449984 | tf_op jit(solution)/shard_map/dot_general | solution.py:502
  137.0 23.8 %home_exchange.1 = bf16[128,1024]{1,0:T(8,128)(2,1)} custom-call(bf16[8,128,128]{2,1,0:T(8,128)(2,1)} %bitcast.27), custom_call_target="tpu_custom_call" | custom-call | tf_op jit(solution)/shard_map/home_exchange/pallas_call | solution.py:449
  160.8 2.6 %fusion.12 = bf16[128,1024]{1,0:T(8,128)(2,1)} fusion(bf16[128,1024]{1,0:T(8,128)(2,1)} %home_exchange.1, s32[1024]{0:T(1024)S(1)} %fusion.39), kind=kOutput, calls=%fused_computation.16 | convolution fusion | flops 269615104 | bytes 528384 | tf_op jit(solution)/shard_map/dot_general | solution.py:505
  (5 shorter events, 0.0 us)
Async XLA Ops:
  0.0 3.0 %copy-start = (bf16[128,1024]{1,0:T(8,128)(2,1)S(1)}, bf16[128,1024]{1,0:T(8,128)(2,1)}, u32[]{:S(2)}) copy-start(bf16[128,1024]{1,0:T(8,128)(2,1)} %param.7) | copy-start | bytes 786436
  131.5 3.0 %copy-start.1 = (bf16[32,80,128]{2,1,0:T(8,128)(2,1)S(1)}, bf16[32,80,128]{2,1,0:T(8,128)(2,1)}, u32[]{:S(2)}) copy-start(bf16[32,80,128]{2,1,0:T(8,128)(2,1)} %get-tuple-element.8) | copy-start | bytes 1966084

commit v3 on v2

--- a/solution.py
+++ b/solution.py
@@ -61,19 +61,20 @@
 
         lax.fori_loop(1, pos.nx * pos.ny, body, 0)
         n += pos.nx * pos.ny - 1
-    pl.semaphore_wait(barrier, n)
+    return n
 
 
 def relay_kernel(pos, dims, refs):
     nx, ny, nz = pos.nx, pos.ny, pos.nz
     nxy = nx * ny
-    parts, cap8, piece, top = dims["parts"], dims["rows"], dims["piece"], dims["top"]
-    depth, lane = dims["depth"], dims["lane"]
-    rows = cap8
+    parts, rows, piece, top = dims["parts"], dims["rows"], dims["piece"], dims["top"]
+    depth, lane, tok, cap = dims["depth"], dims["lane"], dims["tok"], dims["cap"]
+    feats = nz * piece
     half = nx * lane // 2
-    (tok_ref, meta_ref, wg_ref, wu_ref, wd_ref, back_ref, info_ref) = refs[:7]
-    (raw, out_tok, x_in, wbuf, part, land, hid, acc, out) = refs[7:16]
-    (zsend, zrecv, loc, wsend, wrecv, fsend, frecv, tsend, trecv, rsend, rrecv, asend, arecv, bsem) = refs[16:]
+    (count_ref, tokens_ref, lines_ref, wg_ref, wu_ref, wd_ref, final_ref) = refs[:7]
+    (tok_ref, meta_ref, perm, columns, info_ref, back_ref, back_wide, mixed, home) = refs[7:16]
+    (raw, out_tok, x_in, wbuf, part, land, hid, acc, out) = refs[16:25]
+    (zsend, zrecv, loc, wsend, wrecv, fsend, frecv, tsend, trecv, rsend, rrecv, asend, arecv, bsem, hsem) = refs[25:]
     me = pos.here()
     x, y, z, c = me
     weights = (wg_ref, wu_ref, wd_ref)
@@ -85,7 +86,32 @@
     def wait(ref, sem):
         pltpu.make_async_copy(ref, ref, sem).wait()
 
-    signal_all(pos, x, y, z, c, pltpu.get_barrier_semaphore(), True, "all", True)
+    barrier = pltpu.get_barrier_semaphore()
+    partners = signal_all(pos, x, y, z, c, barrier, True, "all", True)
+
+    nzl = pos.nzl
+    new = lax.broadcasted_iota(jnp.int32, (feats, 1), 0)
+    at_z, rest = new // piece, lax.rem(new, piece)
+    ylo, core, row = rest // (2 * depth), lax.rem(rest // depth, 2), lax.rem(rest, depth)
+    old = (((ylo * pos.nzh + at_z // nzl) * 2 + core) * nzl + lax.rem(at_z, nzl)) * depth + row
+    perm[...] = jnp.where(lax.broadcasted_iota(jnp.int32, (feats, feats), 1) == old, 1.0, 0.0).astype(BF16)
+    tok_ref[...] = lax.dot_general(
+        tokens_ref[...], perm[...], (((1,), (1,)), ((), ())), preferred_element_type=F32
+    ).astype(BF16)
+
+    experts = nxy
+    expert_ids = lax.broadcasted_iota(jnp.int32, (experts, tok), 0).astype(F32)
+    live = lax.broadcasted_iota(jnp.int32, (experts, tok), 1) < count_ref[0]
+    named = [(expert_ids == lines_ref[s : s + 1, :]) & live for s in range(top)]
+    either = jnp.where(functools.reduce(jnp.logical_or, named), 1.0, 0.0).astype(BF16)
+    sooner = lax.broadcasted_iota(jnp.int32, (tok, tok), 0) < lax.broadcasted_iota(jnp.int32, (tok, tok), 1)
+    rank = jnp.dot(either, jnp.where(sooner, 1.0, 0.0).astype(BF16), preferred_element_type=F32)
+    meta_ref[...] = lines_ref[...]
+    for s in range(top):
+        place = jnp.where(named[s], expert_ids * cap + rank + 1.0, 0.0)
+        meta_ref[s : s + 1, :] = jnp.sum(place, axis=0, keepdims=True) - 1.0
+
+    pl.semaphore_wait(barrier, partners)
 
     def raw_send(k, carry):
         zz = lax.rem(z + k, nz)
@@ -149,7 +175,7 @@
         for zz in range(nz):
             hit = None
             for s in range(top):
-                same = ids == (info_ref[zz, s : s + 1, :] - base)
+                same = ids == (info_ref[zz, s : s + 1, :] * nz + (zz - base))
                 hit = same if hit is None else hit | same
             picks.append(jnp.where(hit, 1.0, 0.0).astype(BF16))
         pick = jnp.concatenate(picks, axis=1)
@@ -181,6 +207,9 @@
     own_tok = pltpu.make_async_copy(out_tok.at[y * nx + x], t_dst(x, y), loc.at[11])
     own_tok.start()
     w_forward(0, (0, 1))
+
+    for zz in range(nz):
+        columns[zz] = jnp.transpose(info_ref[zz])
 
     def product(w):
         wide = nx * lane
@@ -354,6 +383,39 @@
     finish_rows([at(0, 4)])
     send_rows([at(0, 3), at(1, 3), at(0, 4)])
 
+    pltpu.make_async_copy(o_src(x, y), back_ref.at[y * nx + x], bsem.at[2]).wait()
+    wait(back_ref.at[pl.ds(0, nxy - 1)], bsem.at[1])
+    back_wide[...] = back_ref[...].reshape(nxy * rows, piece).astype(F32)
+    slots = experts * cap
+    slot_ids = lax.broadcasted_iota(jnp.int32, (tok, slots), 1).astype(F32)
+
+    def combine(k):
+        zz = lax.rem(z + k, nz)
+        mine = back_wide[pl.ds(zz, slots, stride=nz), :].astype(BF16)
+        cols = columns[zz]
+        total = jnp.zeros((tok, piece), F32)
+        for s in range(top):
+            chosen = jnp.where(slot_ids == cols[:, s : s + 1], 1.0, 0.0).astype(BF16)
+            total = total + cols[:, top + s : top + s + 1] * jnp.dot(chosen, mine, preferred_element_type=F32)
+        mixed[zz] = total.astype(BF16)
+
+    def home_send(k):
+        zz = lax.rem(z + k, nz)
+        remote(mixed.at[zz], home.at[z], hsem.at[0], hsem.at[1], pos.dev(x, y, zz, c)).start()
+
+    combine(1)
+
+    def home_body(k, carry):
+        combine(k)
+        home_send(k - 1)
+        return carry
+
+    lax.fori_loop(2, nz, home_body, 0)
+    combine(0)
+    home_send(nz - 1)
+    own_home = pltpu.make_async_copy(mixed.at[z], home.at[z], hsem.at[2])
+    own_home.start()
+
     for m in range(3):
         for w in range(parts):
             wait(weights[m].at[pl.ds(0, nxy - 1), :, pl.ds(w * lane, lane)], wsend.at[m, w])
@@ -363,34 +425,46 @@
             for i in range(n):
                 wait(land.at[w, d, h, i], rsend.at[w, d, h, i])
                 wait(hid.at[w, z, :, pl.ds(h * half, half)], asend.at[w, d, h, i])
-    pltpu.make_async_copy(o_src(x, y), back_ref.at[y * nx + x], bsem.at[2]).wait()
     wait(back_ref.at[pl.ds(0, nxy - 1)], bsem.at[0])
-    wait(back_ref.at[pl.ds(0, nxy - 1)], bsem.at[1])
-
-
-def relay(pos, cid, by_z, meta, w_gate, w_up, w_down, cap):
+    own_home.wait()
+    wait(mixed.at[pl.ds(0, nz - 1)], hsem.at[0])
+    wait(home.at[pl.ds(0, nz - 1)], hsem.at[1])
+    merged = jnp.concatenate([home[i] for i in range(nz)], axis=1)
+    final_ref[...] = jnp.dot(merged, perm[...], preferred_element_type=F32).astype(BF16)
+
+
+def relay(pos, cid, token_count, tokens, lines, w_gate, w_up, w_down, cap):
     nx, ny, nz = pos.nx, pos.ny, pos.nz
     nxy = nx * ny
     _, depth, width = w_gate.shape
-    tok, feats = by_z.shape
+    tok, feats = tokens.shape
     piece = feats // nz
     lane = 128
     parts = width // lane
     rows = nz * cap
     wide = nx * lane
-    dims = {"parts": parts, "rows": rows, "piece": piece, "top": 2, "depth": depth, "lane": lane}
+    dims = {
+        "parts": parts, "rows": rows, "piece": piece, "top": 2, "depth": depth, "lane": lane, "tok": tok, "cap": cap
+    }
     any_spec = pl.BlockSpec(memory_space=pl.ANY)
     vmem = pl.BlockSpec(memory_space=pltpu.VMEM)
+    smem = pl.BlockSpec(memory_space=pltpu.SMEM)
     dma = pltpu.SemaphoreType.DMA
     return pl.pallas_call(
         lambda *refs: relay_kernel(pos, dims, refs),
-        out_shape=[
-            jax.ShapeDtypeStruct((nxy, rows, piece), BF16),
-            jax.ShapeDtypeStruct((nz, *meta.shape), F32),
-        ],
-        in_specs=[vmem, vmem, any_spec, any_spec, any_spec],
-        out_specs=[vmem, vmem],
+        out_shape=jax.ShapeDtypeStruct((tok, feats), BF16),
+        in_specs=[smem, vmem, vmem, any_spec, any_spec, any_spec],
+        out_specs=vmem,
         scratch_shapes=[
+            pltpu.VMEM((tok, feats), BF16),
+            pltpu.VMEM((8, tok), F32),
+            pltpu.VMEM((feats, feats), BF16),
+            pltpu.VMEM((nz, tok, 8), F32),
+            pltpu.VMEM((nz, 8, tok), F32),
+            pltpu.VMEM((nxy, rows, piece), BF16),
+            pltpu.VMEM((nxy * rows, piece), F32),
+            pltpu.VMEM((nz, tok, piece), BF16),
+            pltpu.VMEM((nz, tok, piece), BF16),
             pltpu.VMEM((nz, tok, piece), BF16),
             pltpu.VMEM((nxy, rows, piece), BF16),
             pltpu.VMEM((ny, rows, nx * piece), BF16),
@@ -414,95 +488,21 @@
             dma((parts, 2, 2, nz // 2)),
             dma((parts, 2, 2, nz // 2)),
             dma((3,)),
+            dma((3,)),
         ],
         compiler_params=pltpu.CompilerParams(
             collective_id=cid, has_side_effects=True, vmem_limit_bytes=56 * 1024 * 1024
         ),
         name="relay",
-    )(by_z, meta, w_gate, w_up, w_down)
-
-
-def home_exchange(pos, cid, mixed):
-    nz, tok, piece = mixed.shape
-
-    def kernel(src, dst, sems):
-        x, y, z, c = pos.here()
-        signal_all(pos, x, y, z, c, pltpu.get_barrier_semaphore(), False, "all", False)
-        cols = dst.at[:, pl.ds(pl.multiple_of(z * piece, piece), piece)]
-
-        def body(k, carry):
-            zz = lax.rem(z + k, nz)
-            pltpu.make_async_remote_copy(
-                src.at[zz], cols, sems.at[0], sems.at[1], device_id=pos.dev(x, y, zz, c), device_id_type=MESH
-            ).start()
-            return carry
-
-        lax.fori_loop(1, nz, body, 0)
-        own = pltpu.make_async_copy(src.at[z], cols, sems.at[2])
-        own.start()
-        own.wait()
-        part = src.at[pl.ds(0, nz - 1)]
-        pltpu.make_async_copy(part, part, sems.at[0]).wait()
-        pltpu.make_async_copy(part, part, sems.at[1]).wait()
-
-    vmem = pl.BlockSpec(memory_space=pltpu.VMEM)
-    return pl.pallas_call(
-        kernel,
-        out_shape=jax.ShapeDtypeStruct((tok, nz * piece), mixed.dtype),
-        in_specs=[vmem],
-        out_specs=vmem,
-        scratch_shapes=[pltpu.SemaphoreType.DMA((3,))],
-        compiler_params=pltpu.CompilerParams(collective_id=cid, has_side_effects=True),
-        name="home_exchange",
-    )(mixed)
+    )(token_count, tokens, lines, w_gate, w_up, w_down)
 
 
 def shards(pos, tokens, routes, gate_prob, token_count, gate_weight, up_weight, down_weight):
-    experts, depth, _ = gate_weight.shape
-    nz, nzl = pos.nz, pos.nzl
-    nzh = nz // nzl
-    tok, feats = tokens.shape
-    top = routes.shape[1]
+    experts = gate_weight.shape[0]
+    tok, top = routes.shape
     cap = min(tok, tok * top * 5 // (4 * experts))
-    piece = feats // nz
-
-    new = jnp.arange(feats, dtype=jnp.int32)
-    zz, rest = new // piece, new % piece
-    ylo, core, row = rest // (2 * depth), rest // depth % 2, rest % depth
-    old = (((ylo * nzh + zz // nzl) * 2 + core) * nzl + zz % nzl) * depth + row
-    shuffle = (jnp.arange(feats, dtype=jnp.int32)[:, None] == old[None, :]).astype(BF16)
-    by_z = jnp.dot(tokens, shuffle, preferred_element_type=F32).astype(BF16)
-
-    x, y, z, c = pos.here()
-    positions = jnp.arange(tok, dtype=jnp.int32)
-    live = positions < token_count[0]
-    names = routes.T
-    expert_ids = jnp.arange(experts, dtype=jnp.int32)
-    named = [(expert_ids[:, None] == names[s][None, :]) & live[None, :] for s in range(top)]
-    either = functools.reduce(jnp.logical_or, named).astype(BF16)
-    earlier = (positions[:, None] < positions[None, :]).astype(BF16)
-    rank = jnp.dot(either, earlier, preferred_element_type=F32).astype(jnp.int32)
-    lines = []
-    for s in range(top):
-        place = (expert_ids[:, None] * nz + z) * cap + rank
-        lines.append(jnp.sum(jnp.where(named[s], place + 1, 0), axis=0).astype(F32) - 1.0)
-    lines += [gate_prob[:, s] for s in range(top)]
-    meta = jnp.concatenate([jnp.stack(lines), jnp.zeros((8 - 2 * top, tok), F32)])
-
-    back, infos = relay(pos, 1, by_z, meta, gate_weight, up_weight, down_weight, cap)
-
-    slots_all = experts * nz * cap
-    slot_of = [infos[:, s].astype(jnp.int32).reshape(nz * tok) for s in range(top)]
-    slot_ids = jnp.arange(slots_all, dtype=jnp.int32)
-    back = back.reshape(slots_all, piece)
-    mixed = jnp.zeros((nz * tok, piece), F32)
-    for s in range(top):
-        chosen = (slot_of[s][:, None] == slot_ids[None, :]).astype(BF16)
-        prob = infos[:, top + s].reshape(nz * tok)
-        mixed = mixed + prob[:, None] * jnp.dot(chosen, back, preferred_element_type=F32)
-    merged = home_exchange(pos, 2, mixed.astype(BF16).reshape(nz, tok, piece))
-    unshuffle = (old[:, None] == jnp.arange(feats, dtype=jnp.int32)[None, :]).astype(BF16)
-    return jnp.dot(merged, unshuffle, preferred_element_type=F32).astype(BF16)
+    lines = jnp.concatenate([routes.astype(F32), gate_prob, jnp.zeros((tok, 8 - 2 * top), F32)], axis=1).T
+    return relay(pos, 1, token_count, tokens, lines, gate_weight, up_weight, down_weight, cap)
 
 
 def solution(mesh):

time: 164 us -> 151 us (0.921)
  matrix products: 9.8 us -> 0 us
  Pallas kernels: 150 us -> 145 us
    dot_general x5 -> x0, matrix products: 9.8 us -> none  [the longest x2 5.48 us: shards(): jnp.dot(chosen, back, preferred_element_type=F32)]
    pallas_call x2 -> x1, Pallas kernels: 150 us -> 145 us  [relay(): pl.pallas_call(lambda *refs: relay_kernel(pos, dims, refs), out_shape=jax...]
    unnamed x4 -> x5, local copies, waits for them, and re-layouts: 0.01 us -> 2.94 us
where the time goes in v3:
time: 151 us; the launch traced here: 149 us
  Pallas kernels  145 us (96%)
  local copies, waits for them, and re-layouts  3.02 us (2%)
    pallas_call x1, Pallas kernels, relay(): pl.pallas_call(lambda *refs: relay_kernel(pos, dims, refs), out_shape=jax...  145 us

profile of v3, /device:TPU:1, one launch (start us, length us, event | category | flops | bytes accessed | tf_op | source)
XLA Modules:
  0.0 149.2 jit_solution(9878427927835105912)
XLA Ops:
  0.7 0.0 copy-start
  0.7 0.1 pad.2.clone
  0.8 0.6 copy-done
  1.3 0.0 copy-start.1
  1.4 0.7 copy-done.1
  2.0 0.7 maximum_bitcast_fusion.refs_2_
  2.7 144.8 %relay.1 = bf16[128,1024]{1,0:T(8,128)(2,1)} custom-call(s32[1]{0:T(128)S(6)} %copy.9.refs_0_, bf16[128,1024]{1,0:T(8,128)(2,1)} %refs_1_.1, f32[8,128]{1,0:T(8,128)} %maximum_bitcast_fusion.refs_2_, bf16[32,32,384]{2,1,0:T(8,128)(2,1)} %refs_3_.1, bf16[32,32,384]{2,1,0:T(8,128)(2,1)} %refs_4_.1, bf16[32,32,384]{2,1,0:T(8,128)(2,1)} %refs_5_.1), custom_call_target="tpu_custom_call" | custom-call | tf_op jit(solution)/shard_map/relay/pallas_call | solution.py:453
  147.5 1.7 %copy.10 = bf16[128,1024]{1,0:T(8,128)(2,1)} copy(bf16[128,1024]{1,0:T(8,128)(2,1)} %relay.1) | data formatting | bytes 524288
  (2 shorter events, 0.0 us)
Async XLA Ops:
  0.7 0.7 copy-start
  1.3 0.7 copy-start.1

commit v4 on v3

--- a/solution.py
+++ b/solution.py
@@ -71,10 +71,10 @@
     depth, lane, tok, cap = dims["depth"], dims["lane"], dims["tok"], dims["cap"]
     feats = nz * piece
     half = nx * lane // 2
-    (count_ref, tokens_ref, lines_ref, wg_ref, wu_ref, wd_ref, final_ref) = refs[:7]
-    (tok_ref, meta_ref, perm, columns, info_ref, back_ref, back_wide, mixed, home) = refs[7:16]
-    (raw, out_tok, x_in, wbuf, part, land, hid, acc, out) = refs[16:25]
-    (zsend, zrecv, loc, wsend, wrecv, fsend, frecv, tsend, trecv, rsend, rrecv, asend, arecv, bsem, hsem) = refs[25:]
+    (count_ref, tokens_ref, names_ref, prob_ref, wg_ref, wu_ref, wd_ref, final_ref) = refs[:8]
+    (tok_ref, meta_ref, perm, columns, info_ref, back_ref, back_wide, mixed, home) = refs[8:17]
+    (raw, out_tok, x_in, wbuf, part, land, hid, perm_back, out) = refs[17:26]
+    (zsend, zrecv, loc, wsend, wrecv, fsend, frecv, tsend, trecv, rsend, rrecv, asend, arecv, bsem, hsem) = refs[26:]
     me = pos.here()
     x, y, z, c = me
     weights = (wg_ref, wu_ref, wd_ref)
@@ -89,41 +89,51 @@
     barrier = pltpu.get_barrier_semaphore()
     partners = signal_all(pos, x, y, z, c, barrier, True, "all", True)
 
-    nzl = pos.nzl
-    new = lax.broadcasted_iota(jnp.int32, (feats, 1), 0)
-    at_z, rest = new // piece, lax.rem(new, piece)
-    ylo, core, row = rest // (2 * depth), lax.rem(rest // depth, 2), lax.rem(rest, depth)
-    old = (((ylo * pos.nzh + at_z // nzl) * 2 + core) * nzl + lax.rem(at_z, nzl)) * depth + row
-    perm[...] = jnp.where(lax.broadcasted_iota(jnp.int32, (feats, feats), 1) == old, 1.0, 0.0).astype(BF16)
-    tok_ref[...] = lax.dot_general(
-        tokens_ref[...], perm[...], (((1,), (1,)), ((), ())), preferred_element_type=F32
-    ).astype(BF16)
+    nzl, nzh = pos.nzl, pos.nzh
+    nseg = piece // depth
+    block = nzl * depth
+    lanes = lax.broadcasted_iota(jnp.int32, (1, nzl * piece), 1)
+    inner = lax.rem(lanes, piece)
+    source = (inner // depth) * block + (lanes // piece) * depth + lax.rem(inner, depth)
+    ids = lax.broadcasted_iota(jnp.int32, (nseg * block, nzl * piece), 0)
+    perm[...] = jnp.where(ids == source, 1.0, 0.0).astype(BF16)
+
+    def blocks_of(zh):
+        return [pl.ds((((seg // 2) * nzh + zh) * 2 + seg % 2) * block, block) for seg in range(nseg)]
+
+    for zh in range(nzh):
+        left = jnp.concatenate([tokens_ref[:, b] for b in blocks_of(zh)], axis=1)
+        got = jnp.dot(left, perm[...], preferred_element_type=F32).astype(BF16)
+        for zl in range(nzl):
+            tok_ref[zh * nzl + zl] = got[:, zl * piece : (zl + 1) * piece]
 
     experts = nxy
-    expert_ids = lax.broadcasted_iota(jnp.int32, (experts, tok), 0).astype(F32)
+    expert_ids = lax.broadcasted_iota(jnp.int32, (experts, tok), 0)
     live = lax.broadcasted_iota(jnp.int32, (experts, tok), 1) < count_ref[0]
-    named = [(expert_ids == lines_ref[s : s + 1, :]) & live for s in range(top)]
+    named = [(expert_ids == names_ref[s : s + 1, :]) & live for s in range(top)]
     either = jnp.where(functools.reduce(jnp.logical_or, named), 1.0, 0.0).astype(BF16)
     sooner = lax.broadcasted_iota(jnp.int32, (tok, tok), 0) < lax.broadcasted_iota(jnp.int32, (tok, tok), 1)
     rank = jnp.dot(either, jnp.where(sooner, 1.0, 0.0).astype(BF16), preferred_element_type=F32)
-    meta_ref[...] = lines_ref[...]
+    meta_ref[...] = jnp.zeros_like(meta_ref)
+    meta_ref[top : 2 * top, :] = prob_ref[...]
     for s in range(top):
-        place = jnp.where(named[s], expert_ids * cap + rank + 1.0, 0.0)
+        place = jnp.where(named[s], (expert_ids * cap).astype(F32) + rank + 1.0, 0.0)
         meta_ref[s : s + 1, :] = jnp.sum(place, axis=0, keepdims=True) - 1.0
 
     pl.semaphore_wait(barrier, partners)
 
-    def raw_send(k, carry):
-        zz = lax.rem(z + k, nz)
+    def far_first(i):
+        return nz // 2 + (1 - 2 * lax.rem(i, 2)) * ((i + 1) // 2)
+
+    def raw_send(i, carry):
+        zz = lax.rem(z + far_first(i), nz)
         dev = pos.dev(x, y, zz, c)
-        cols = pl.ds(pl.multiple_of(zz * piece, piece), piece)
+        remote(tok_ref.at[zz], raw.at[z], zsend.at[0], zrecv.at[0], dev).start()
         remote(meta_ref, info_ref.at[z], zsend.at[1], zrecv.at[1], dev).start()
-        remote(tok_ref.at[:, cols], raw.at[z], zsend.at[0], zrecv.at[0], dev).start()
         return carry
 
-    lax.fori_loop(1, nz, raw_send, 0)
-    own_cols = pl.ds(pl.multiple_of(z * piece, piece), piece)
-    own_raw = pltpu.make_async_copy(tok_ref.at[:, own_cols], raw.at[z], loc.at[0])
+    lax.fori_loop(0, nz - 1, raw_send, 0)
+    own_raw = pltpu.make_async_copy(tok_ref.at[z], raw.at[z], loc.at[0])
     own_meta = pltpu.make_async_copy(meta_ref, info_ref.at[z], loc.at[1])
     own_raw.start()
     own_meta.start()
@@ -167,8 +177,11 @@
         wait(ref.at[pl.ds(0, nz - 1)], zrecv.at[i])
     count = nx * rows
 
-    def dispatch(dy):
-        yy = lax.rem(y + dy, ny)
+    def dy_of(i):
+        return lax.rem(3 * nz - z - far_first(i), nz)
+
+    def dispatch(i):
+        yy = lax.rem(y + dy_of(i), ny)
         ids = lax.broadcasted_iota(jnp.int32, (count, raw.shape[1]), 0).astype(F32)
         base = (yy * count).astype(F32)
         picks = []
@@ -179,37 +192,90 @@
                 hit = same if hit is None else hit | same
             picks.append(jnp.where(hit, 1.0, 0.0).astype(BF16))
         pick = jnp.concatenate(picks, axis=1)
-        feats = raw[...].reshape(nz * raw.shape[1], piece)
-        got = jnp.dot(pick, feats, preferred_element_type=F32).astype(BF16)
+        got = jnp.dot(pick, raw[...].reshape(nz * tok, piece), preferred_element_type=F32).astype(BF16)
         out_tok[pl.ds(yy * nx, nx)] = got.reshape(nx, rows, piece)
 
     def t_dst(xs, ys):
         return x_in.at[ys, :, pl.ds(pl.multiple_of(xs * piece, piece), piece)]
 
-    def t_send(dy, first):
+    def t_send(i):
+        dy = dy_of(i)
         yy = lax.rem(y + dy, ny)
-        for dx in range(first, nx):
+        for dx in range(nx):
             xx = lax.rem(x + dx, nx)
-            remote(out_tok.at[yy * nx + xx], t_dst(x, y), tsend, trecv, pos.dev(xx, yy, z, c)).start()
-
-    dispatch(1)
-
-    def d_body(dy, carry):
-        dispatch(dy)
-        t_send(dy - 1, 0)
+            away = remote(out_tok.at[yy * nx + xx], t_dst(x, y), tsend.at[i], trecv.at[dy], pos.dev(xx, yy, z, c))
+            if dx:
+                away.start()
+            else:
+
+                @pl.when(dy != 0)
+                def _():
+                    away.start()
+
+                @pl.when(dy == 0)
+                def _():
+                    pltpu.make_async_copy(out_tok.at[y * nx + x], t_dst(x, y), loc.at[11]).start()
+
+    def t_sent(i):
+        dy = dy_of(i)
+
+        @pl.when(dy == 0)
+        def _():
+            wait(out_tok.at[pl.ds(0, nx - 1)], tsend.at[i])
+
+        @pl.when(dy != 0)
+        def _():
+            wait(out_tok.at[pl.ds(0, nx)], tsend.at[i])
+
+    dispatch(0)
+
+    def d_body(i, carry):
+        dispatch(i)
+        t_send(i - 1)
         return carry
 
-    lax.fori_loop(2, ny, d_body, 0)
-    dispatch(0)
-    t_send(ny - 1, 0)
-    w_start(1, (0, 1))
-    t_send(0, 1)
-    own_tok = pltpu.make_async_copy(out_tok.at[y * nx + x], t_dst(x, y), loc.at[11])
-    own_tok.start()
-    w_forward(0, (0, 1))
-
+    lax.fori_loop(1, 5, d_body, 0)
+
+    def d_late(i, carry):
+        dispatch(i)
+        t_sent(i - 5)
+        t_send(i - 1)
+        return carry
+
+    lax.fori_loop(5, ny, d_late, 0)
     for zz in range(nz):
         columns[zz] = jnp.transpose(info_ref[zz])
+    lanes = lax.broadcasted_iota(jnp.int32, (1, nseg * block), 1)
+    inner = lax.rem(lanes, block)
+    source = (inner // depth) * piece + (lanes // block) * depth + lax.rem(inner, depth)
+    ids = lax.broadcasted_iota(jnp.int32, (nzl * piece, nseg * block), 0)
+    perm_back[...] = jnp.where(ids == source, 1.0, 0.0).astype(BF16)
+    t_sent(3)
+    t_send(ny - 1)
+    w_forward(0, (0, 1))
+    t_sent(4)
+    t_sent(5)
+    w_start(1, (0, 1))
+
+    def token_wait(i):
+        dy = dy_of(i)
+
+        @pl.when(dy == 0)
+        def _():
+            pltpu.make_async_copy(out_tok.at[y * nx + x], t_dst(x, y), loc.at[11]).wait()
+            wait(x_in.at[0, :, pl.ds(0, (nx - 1) * piece)], trecv.at[0])
+
+        @pl.when(dy != 0)
+        def _():
+            wait(x_in.at[0], trecv.at[dy])
+
+    def first_part(order):
+        js = [lax.rem(z + y + far_first(i), nz) for i in order]
+        left = jnp.concatenate([x_in[j] for j in js], axis=0) if len(js) > 1 else x_in[js[0]]
+        for m in range(2):
+            res = jnp.dot(left, wbuf[0, m].reshape(ny * 2 * depth, nx * lane), preferred_element_type=F32).astype(BF16)
+            for i, j in enumerate(js):
+                part[0, j, :, m * nx * lane : (m + 1) * nx * lane] = res[i * rows : (i + 1) * rows]
 
     def product(w):
         wide = nx * lane
@@ -230,8 +296,10 @@
     chains = [(d, h, far if h == d else far - 1) for h in range(2) for d in range(2)]
     wide = nx * lane
 
+    mine_at = lax.rem(z + y, nz)
+
     def at(d, k):
-        return lax.rem(z + (k if d == 0 else -k) + 2 * nz, nz)
+        return lax.rem(mine_at + (k if d == 0 else -k) + 2 * nz, nz)
 
     def rs_send(w, d, h, i, src):
         remote(src, land.at[w, d, h, i], rsend.at[w, d, h, i], rrecv.at[w, d, h, i], near[d]).start()
@@ -241,24 +309,32 @@
             rs_send(w, d, h, 0, part.at[w, at(d, n), :, pl.ds(h * wide, wide)])
 
     def rs_mid(w, i):
+        ready = None
         for d, h, n in chains:
             if i < n:
                 slot = land.at[w, d, h, i - 1]
                 wait(slot, rrecv.at[w, d, h, i - 1])
                 mine = part[w, at(d, n - i), :, pl.ds(h * wide, wide)]
                 slot[...] = (slot[...].astype(F32) + mine.astype(F32)).astype(BF16)
-        for d, h, n in chains:
-            if i < n:
-                rs_send(w, d, h, i, land.at[w, d, h, i - 1])
-
-    def ag_send(w, d, h, i, j):
-        block = hid.at[w, j, :, pl.ds(h * half, half)]
-        remote(block, block, asend.at[w, d, h, i], arecv.at[w, d, h, i], near[d]).start()
+                if ready is not None:
+                    rs_send(w, *ready)
+                ready = (d, h, i, slot)
+        if ready is not None:
+            rs_send(w, *ready)
+
+    cuts = ((0, 48), (48, rows - 48))
+
+    def hid_cut(w, j, h, p):
+        return hid.at[w, j, pl.ds(*cuts[p]), pl.ds(h * half, half)]
+
+    def ag_send(w, d, h, i, j, p):
+        block = hid_cut(w, j, h, p)
+        remote(block, block, asend.at[w, d, h, i, p], arecv.at[w, d, h, i, p], near[d]).start()
 
     def rs_final(w):
         total = []
         for h in range(2):
-            t = part[w, z, :, pl.ds(h * wide, wide)].astype(F32)
+            t = part[w, mine_at, :, pl.ds(h * wide, wide)].astype(F32)
             for d, hh, n in chains:
                 if hh == h:
                     slot = land.at[w, d, h, n - 1]
@@ -266,43 +342,34 @@
                     t = t + slot[...].astype(F32)
             total.append(t)
         gate, up = total
-        hid[w, z] = (gate / (1.0 + jnp.exp(-gate)) * up).astype(BF16)
+        hid[w, mine_at] = (gate / (1.0 + jnp.exp(-gate)) * up).astype(BF16)
 
     def ag_start(w):
-        for d, h, n in chains:
-            ag_send(w, d, h, 0, z)
+        for p in range(len(cuts)):
+            for d, h, n in chains:
+                ag_send(w, d, h, 0, mine_at, p)
 
     def ag_mid(w, i):
-        for d, h, n in chains:
-            if i <= n:
-                j = at(d, -i)
-                wait(hid.at[w, j, :, pl.ds(h * half, half)], arecv.at[w, d, h, i - 1])
-                if i < n:
-                    ag_send(w, d, h, i, j)
-
-    def down(w, left):
-        return lax.dot_general(
-            left, wbuf[w, 2].reshape(ny * 2 * depth, wide), (((1,), (1,)), ((), ())), preferred_element_type=F32
-        )
-
-    def accumulate(w):
-        def body(i, carry):
-            span = pl.ds(i * (nz // 2), nz // 2)
-            res = down(w, hid[w, span].reshape(nz // 2 * rows, wide)).reshape(nz // 2, rows, ny * 2 * depth)
-            acc[span] = res if w == 0 else acc[span] + res
-            return carry
-
-        lax.fori_loop(0, 2, body, 0)
+        for p in range(len(cuts)):
+            for d, h, n in chains:
+                if i <= n:
+                    j = at(d, -i)
+                    wait(hid_cut(w, j, h, p), arecv.at[w, d, h, i - 1, p])
+                    if i < n:
+                        ag_send(w, d, h, i, j, p)
 
     def o_src(xx, j):
         return out.at[j, :, pl.ds(pl.multiple_of(xx * piece, piece), piece)]
 
     def finish_rows(js):
-        last = parts - 1
-        left = jnp.concatenate([hid[last, j] for j in js], axis=0) if len(js) > 1 else hid[last, js[0]]
-        res = down(last, left)
+        res = None
+        for w in range(parts):
+            left = jnp.concatenate([hid[w, j] for j in js], axis=0) if len(js) > 1 else hid[w, js[0]]
+            right = wbuf[w, 2].reshape(ny * 2 * depth, wide)
+            more = lax.dot_general(left, right, (((1,), (1,)), ((), ())), preferred_element_type=F32)
+            res = more if res is None else res + more
         for i, j in enumerate(js):
-            out[j] = (acc[j] + res[i * rows : (i + 1) * rows]).astype(BF16)
+            out[j] = res[i * rows : (i + 1) * rows].astype(BF16)
 
     def send_rows(js):
         for j in js:
@@ -321,26 +388,35 @@
                     def _():
                         pltpu.make_async_copy(o_src(x, y), back_ref.at[y * nx + x], bsem.at[2]).start()
 
-    own_tok.wait()
-    wait(out_tok.at[pl.ds(0, nxy - 1)], tsend)
-    wait(out_tok.at[pl.ds(0, nxy - 1)], trecv)
     w_ready(0, (0, 1))
-    product(0)
+    token_wait(0)
+    token_wait(1)
+    token_wait(2)
+    first_part([0])
+    first_part([1, 2])
     rs_start(0)
+    token_wait(3)
+    token_wait(4)
+    first_part([3, 4])
+    rs_mid(0, 1)
+    token_wait(5)
+    token_wait(6)
+    first_part([5, 6])
+    token_wait(7)
+    first_part([7])
     w_start(2, (0, 1))
-    rs_mid(0, 1)
+    rs_mid(0, 2)
     w_forward(1, (0, 1))
-    rs_mid(0, 2)
+    rs_mid(0, 3)
     w_ready(1, (0, 1))
     product(1)
     rs_start(1)
     for w in range(parts):
         w_start(w, (2,))
-    rs_mid(0, 3)
+    rs_final(0)
+    ag_start(0)
     rs_mid(1, 1)
-    rs_final(0)
     w_forward(2, (0, 1))
-    ag_start(0)
     rs_mid(1, 2)
     w_ready(2, (0, 1))
     product(2)
@@ -358,30 +434,29 @@
     rs_mid(2, 3)
     ag_mid(0, 4)
     ag_mid(1, 2)
+    w_forward(1, (2,))
+    w_forward(2, (2,))
     w_ready(0, (2,))
-    accumulate(0)
     rs_final(2)
-    w_forward(1, (2,))
     ag_start(2)
-    ag_mid(1, 3)
-    w_forward(2, (2,))
-    ag_mid(1, 4)
     w_ready(1, (2,))
     w_ready(2, (2,))
+    finish_rows([mine_at])
+    send_rows([mine_at])
+    ag_mid(1, 3)
     ag_mid(2, 1)
-    accumulate(1)
-    finish_rows([z])
+    finish_rows([at(0, 1), at(1, 1)])
+    send_rows([at(0, 1), at(1, 1)])
+    ag_mid(1, 4)
     ag_mid(2, 2)
-    finish_rows([at(0, 1), at(1, 1)])
-    send_rows([z])
+    finish_rows([at(0, 2), at(1, 2)])
+    send_rows([at(0, 2), at(1, 2)])
     ag_mid(2, 3)
-    finish_rows([at(0, 2), at(1, 2)])
-    send_rows([at(0, 1), at(1, 1)])
+    finish_rows([at(0, 3), at(1, 3)])
+    send_rows([at(0, 3), at(1, 3)])
     ag_mid(2, 4)
-    finish_rows([at(0, 3), at(1, 3)])
-    send_rows([at(0, 2), at(1, 2)])
     finish_rows([at(0, 4)])
-    send_rows([at(0, 3), at(1, 3), at(0, 4)])
+    send_rows([at(0, 4)])
 
     pltpu.make_async_copy(o_src(x, y), back_ref.at[y * nx + x], bsem.at[2]).wait()
     wait(back_ref.at[pl.ds(0, nxy - 1)], bsem.at[1])
@@ -389,8 +464,8 @@
     slots = experts * cap
     slot_ids = lax.broadcasted_iota(jnp.int32, (tok, slots), 1).astype(F32)
 
-    def combine(k):
-        zz = lax.rem(z + k, nz)
+    def combine(i):
+        zz = lax.rem(z + far_first(i), nz)
         mine = back_wide[pl.ds(zz, slots, stride=nz), :].astype(BF16)
         cols = columns[zz]
         total = jnp.zeros((tok, piece), F32)
@@ -399,20 +474,18 @@
             total = total + cols[:, top + s : top + s + 1] * jnp.dot(chosen, mine, preferred_element_type=F32)
         mixed[zz] = total.astype(BF16)
 
-    def home_send(k):
-        zz = lax.rem(z + k, nz)
+    def home_send(i):
+        zz = lax.rem(z + far_first(i), nz)
         remote(mixed.at[zz], home.at[z], hsem.at[0], hsem.at[1], pos.dev(x, y, zz, c)).start()
 
-    combine(1)
-
-    def home_body(k, carry):
-        combine(k)
-        home_send(k - 1)
+    combine(0)
+
+    def home_body(i, carry):
+        combine(i)
+        home_send(i - 1)
         return carry
 
-    lax.fori_loop(2, nz, home_body, 0)
-    combine(0)
-    home_send(nz - 1)
+    lax.fori_loop(1, nz, home_body, 0)
     own_home = pltpu.make_async_copy(mixed.at[z], home.at[z], hsem.at[2])
     own_home.start()
 
@@ -424,16 +497,22 @@
         for d, h, n in chains:
             for i in range(n):
                 wait(land.at[w, d, h, i], rsend.at[w, d, h, i])
-                wait(hid.at[w, z, :, pl.ds(h * half, half)], asend.at[w, d, h, i])
+                for p in range(len(cuts)):
+                    wait(hid_cut(w, mine_at, h, p), asend.at[w, d, h, i, p])
+    for i in (ny - 2, ny - 1):
+        t_sent(i)
     wait(back_ref.at[pl.ds(0, nxy - 1)], bsem.at[0])
     own_home.wait()
     wait(mixed.at[pl.ds(0, nz - 1)], hsem.at[0])
     wait(home.at[pl.ds(0, nz - 1)], hsem.at[1])
-    merged = jnp.concatenate([home[i] for i in range(nz)], axis=1)
-    final_ref[...] = jnp.dot(merged, perm[...], preferred_element_type=F32).astype(BF16)
-
-
-def relay(pos, cid, token_count, tokens, lines, w_gate, w_up, w_down, cap):
+    for zh in range(nzh):
+        left = jnp.concatenate([home[zh * nzl + zl] for zl in range(nzl)], axis=1)
+        got = jnp.dot(left, perm_back[...], preferred_element_type=F32).astype(BF16)
+        for seg, b in enumerate(blocks_of(zh)):
+            final_ref[:, b] = got[:, seg * block : (seg + 1) * block]
+
+
+def relay(pos, cid, token_count, tokens, names, probs, w_gate, w_up, w_down, cap):
     nx, ny, nz = pos.nx, pos.ny, pos.nz
     nxy = nx * ny
     _, depth, width = w_gate.shape
@@ -453,12 +532,12 @@
     return pl.pallas_call(
         lambda *refs: relay_kernel(pos, dims, refs),
         out_shape=jax.ShapeDtypeStruct((tok, feats), BF16),
-        in_specs=[smem, vmem, vmem, any_spec, any_spec, any_spec],
+        in_specs=[smem, vmem, vmem, vmem, any_spec, any_spec, any_spec],
         out_specs=vmem,
         scratch_shapes=[
-            pltpu.VMEM((tok, feats), BF16),
+            pltpu.VMEM((nz, tok, piece), BF16),
             pltpu.VMEM((8, tok), F32),
-            pltpu.VMEM((feats, feats), BF16),
+            pltpu.VMEM((feats // 2, feats // 2), BF16),
             pltpu.VMEM((nz, tok, 8), F32),
             pltpu.VMEM((nz, 8, tok), F32),
             pltpu.VMEM((nxy, rows, piece), BF16),
@@ -472,7 +551,7 @@
             pltpu.VMEM((parts, nz, rows, 2 * wide), BF16),
             pltpu.VMEM((parts, 2, 2, nz // 2, rows, wide), BF16),
             pltpu.VMEM((parts, nz, rows, wide), BF16),
-            pltpu.VMEM((nz, rows, ny * 2 * depth), F32),
+            pltpu.VMEM((feats // 2, feats // 2), BF16),
             pltpu.VMEM((nz, rows, nx * piece), BF16),
             dma((2,)),
             dma((2,)),
@@ -481,12 +560,12 @@
             dma((3, parts)),
             dma((3, parts)),
             dma((3, parts)),
-            dma,
-            dma,
+            dma((ny,)),
+            dma((ny,)),
             dma((parts, 2, 2, nz // 2)),
             dma((parts, 2, 2, nz // 2)),
-            dma((parts, 2, 2, nz // 2)),
-            dma((parts, 2, 2, nz // 2)),
+            dma((parts, 2, 2, nz // 2, 2)),
+            dma((parts, 2, 2, nz // 2, 2)),
             dma((3,)),
             dma((3,)),
         ],
@@ -494,15 +573,14 @@
             collective_id=cid, has_side_effects=True, vmem_limit_bytes=56 * 1024 * 1024
         ),
         name="relay",
-    )(token_count, tokens, lines, w_gate, w_up, w_down)
+    )(token_count, tokens, names, probs, w_gate, w_up, w_down)
 
 
 def shards(pos, tokens, routes, gate_prob, token_count, gate_weight, up_weight, down_weight):
     experts = gate_weight.shape[0]
     tok, top = routes.shape
     cap = min(tok, tok * top * 5 // (4 * experts))
-    lines = jnp.concatenate([routes.astype(F32), gate_prob, jnp.zeros((tok, 8 - 2 * top), F32)], axis=1).T
-    return relay(pos, 1, token_count, tokens, lines, gate_weight, up_weight, down_weight, cap)
+    return relay(pos, 1, token_count, tokens, routes.T, gate_prob.T, gate_weight, up_weight, down_weight, cap)
 
 
 def solution(mesh):

time: 151 us -> 145 us (0.960)
  Pallas kernels: 145 us -> 142 us
    pallas_call x1, Pallas kernels: 145 us -> 142 us  [relay(): pl.pallas_call(lambda *refs: relay_kernel(pos, dims, refs), out_shape=jax...]
where the time goes in v4:
time: 145 us; the launch traced here: 144 us
  Pallas kernels  142 us (98%)
  local copies, waits for them, and re-layouts  1.67 us (1%)
    pallas_call x1, Pallas kernels, relay(): pl.pallas_call(lambda *refs: relay_kernel(pos, dims, refs), out_shape=jax...  142 us

profile of v4, /device:TPU:1, one launch (start us, length us, event | category | flops | bytes accessed | tf_op | source)
XLA Modules:
  0.0 144.4 jit_solution(5126462406208519045)
XLA Ops:
  0.7 142.0 %relay.1 = bf16[128,1024]{1,0:T(8,128)(2,1)} custom-call(s32[1]{0:T(128)S(6)} %copy.9.refs_0_, bf16[128,1024]{1,0:T(8,128)(2,1)} %refs_1_.1, s32[2,128]{1,0:T(2,128)} %bitcast.2, f32[2,128]{1,0:T(2,128)} %bitcast.3, bf16[32,32,384]{2,1,0:T(8,128)(2,1)} %refs_4_.1, bf16[32,32,384]{2,1,0:T(8,128)(2,1)} %refs_5_.1, bf16[32,32,384]{2,1,0:T(8,128)(2,1)} %refs_6_.1), custom_call_target="tpu_custom_call" | custom-call | tf_op jit(solution)/shard_map/relay/pallas_call | solution.py:532
  142.7 1.7 %copy.10 = bf16[128,1024]{1,0:T(8,128)(2,1)} copy(bf16[128,1024]{1,0:T(8,128)(2,1)} %relay.1) | data formatting | bytes 524288

commit v5 on v4

--- a/solution.py
+++ b/solution.py
@@ -73,8 +73,8 @@
     half = nx * lane // 2
     (count_ref, tokens_ref, names_ref, prob_ref, wg_ref, wu_ref, wd_ref, final_ref) = refs[:8]
     (tok_ref, meta_ref, perm, columns, info_ref, back_ref, back_wide, mixed, home) = refs[8:17]
-    (raw, out_tok, x_in, wbuf, part, land, hid, perm_back, out) = refs[17:26]
-    (zsend, zrecv, loc, wsend, wrecv, fsend, frecv, tsend, trecv, rsend, rrecv, asend, arecv, bsem, hsem) = refs[26:]
+    (raw, out_tok, x_in, wbuf, part, land, hid, perm_back, out, result) = refs[17:27]
+    (zsend, zrecv, loc, wsend, wrecv, fsend, frecv, tsend, trecv, rsend, rrecv, asend, arecv, bsem, hsem) = refs[27:]
     me = pos.here()
     x, y, z, c = me
     weights = (wg_ref, wu_ref, wd_ref)
@@ -150,7 +150,7 @@
             yy = lax.rem(y + k // nx, ny)
             dev = pos.dev(xx, yy, z, c)
             for m in mats:
-                remote(w_src(m, w, yy * nx + xx), w_dst(m, w, x, y, c), wsend.at[m, w], wrecv.at[m, w], dev).start()
+                remote(w_src(m, w, yy * nx + xx), w_dst(m, w, x, y, c), wsend.at[m], wrecv.at[m, w], dev).start()
             return carry
 
         lax.fori_loop(1, nxy, body, 0)
@@ -162,7 +162,7 @@
             pltpu.make_async_copy(w_src(m, w, y * nx + x), w_dst(m, w, x, y, c), loc.at[2 + 3 * w + m]).wait()
             wait(weights[m].at[pl.ds(0, nxy - 1), :, pl.ds(w * lane, lane)], wrecv.at[m, w])
             block = wbuf.at[w, m, :, c]
-            remote(block, block, fsend.at[m, w], frecv.at[m, w], partner).start()
+            remote(block, block, fsend, frecv.at[m, w], partner).start()
 
     def w_ready(w, mats):
         for m in mats:
@@ -269,13 +269,17 @@
         def _():
             wait(x_in.at[0], trecv.at[dy])
 
+    def spot(h, m):
+        return slice((2 * h + m) * half, (2 * h + m + 1) * half)
+
     def first_part(order):
         js = [lax.rem(z + y + far_first(i), nz) for i in order]
         left = jnp.concatenate([x_in[j] for j in js], axis=0) if len(js) > 1 else x_in[js[0]]
         for m in range(2):
             res = jnp.dot(left, wbuf[0, m].reshape(ny * 2 * depth, nx * lane), preferred_element_type=F32).astype(BF16)
             for i, j in enumerate(js):
-                part[0, j, :, m * nx * lane : (m + 1) * nx * lane] = res[i * rows : (i + 1) * rows]
+                for h in range(2):
+                    part[0, j, :, spot(h, m)] = res[i * rows : (i + 1) * rows, h * half : (h + 1) * half]
 
     def product(w):
         wide = nx * lane
@@ -285,7 +289,9 @@
             def body(i, carry):
                 left = x_in[pl.ds(i * (ny // 2), ny // 2)].reshape(ny // 2 * rows, nx * piece)
                 res = jnp.dot(left, right, preferred_element_type=F32).astype(BF16)
-                part[w, pl.ds(i * (ny // 2), ny // 2), :, m * wide : (m + 1) * wide] = res.reshape(ny // 2, rows, wide)
+                span = pl.ds(i * (ny // 2), ny // 2)
+                for h in range(2):
+                    part[w, span, :, spot(h, m)] = res[:, h * half : (h + 1) * half].reshape(ny // 2, rows, half)
                 return carry
 
             lax.fori_loop(0, 2, body, 0)
@@ -302,16 +308,17 @@
         return lax.rem(mine_at + (k if d == 0 else -k) + 2 * nz, nz)
 
     def rs_send(w, d, h, i, src):
-        remote(src, land.at[w, d, h, i], rsend.at[w, d, h, i], rrecv.at[w, d, h, i], near[d]).start()
-
-    def rs_start(w):
+        remote(src, land.at[w, d, h, i], rsend, rrecv.at[w, d, h, i], near[d]).start()
+
+    def rs_start(w, hs=(0, 1)):
         for d, h, n in chains:
-            rs_send(w, d, h, 0, part.at[w, at(d, n), :, pl.ds(h * wide, wide)])
-
-    def rs_mid(w, i):
+            if h in hs:
+                rs_send(w, d, h, 0, part.at[w, at(d, n), :, pl.ds(h * wide, wide)])
+
+    def rs_mid(w, i, hs=(0, 1)):
         ready = None
         for d, h, n in chains:
-            if i < n:
+            if h in hs and i < n:
                 slot = land.at[w, d, h, i - 1]
                 wait(slot, rrecv.at[w, d, h, i - 1])
                 mine = part[w, at(d, n - i), :, pl.ds(h * wide, wide)]
@@ -322,41 +329,35 @@
         if ready is not None:
             rs_send(w, *ready)
 
-    cuts = ((0, 48), (48, rows - 48))
-
-    def hid_cut(w, j, h, p):
-        return hid.at[w, j, pl.ds(*cuts[p]), pl.ds(h * half, half)]
-
-    def ag_send(w, d, h, i, j, p):
-        block = hid_cut(w, j, h, p)
-        remote(block, block, asend.at[w, d, h, i, p], arecv.at[w, d, h, i, p], near[d]).start()
-
-    def rs_final(w):
-        total = []
-        for h in range(2):
-            t = part[w, mine_at, :, pl.ds(h * wide, wide)].astype(F32)
-            for d, hh, n in chains:
-                if hh == h:
-                    slot = land.at[w, d, h, n - 1]
-                    wait(slot, rrecv.at[w, d, h, n - 1])
-                    t = t + slot[...].astype(F32)
-            total.append(t)
-        gate, up = total
-        hid[w, mine_at] = (gate / (1.0 + jnp.exp(-gate)) * up).astype(BF16)
-
-    def ag_start(w):
-        for p in range(len(cuts)):
-            for d, h, n in chains:
-                ag_send(w, d, h, 0, mine_at, p)
-
-    def ag_mid(w, i):
-        for p in range(len(cuts)):
-            for d, h, n in chains:
-                if i <= n:
-                    j = at(d, -i)
-                    wait(hid_cut(w, j, h, p), arecv.at[w, d, h, i - 1, p])
-                    if i < n:
-                        ag_send(w, d, h, i, j, p)
+    def hid_half(w, j, h):
+        return hid.at[w, j, :, pl.ds(h * half, half)]
+
+    def ag_send(w, d, h, i, j):
+        block = hid_half(w, j, h)
+        remote(block, block, asend, arecv.at[w, d, h, i], near[d]).start()
+
+    def rs_final(w, h):
+        total = part[w, mine_at, :, pl.ds(h * wide, wide)].astype(F32)
+        for d, hh, n in chains:
+            if hh == h:
+                slot = land.at[w, d, h, n - 1]
+                wait(slot, rrecv.at[w, d, h, n - 1])
+                total = total + slot[...].astype(F32)
+        gate, up = total[:, :half], total[:, half:]
+        hid[w, mine_at, :, h * half : (h + 1) * half] = (gate / (1.0 + jnp.exp(-gate)) * up).astype(BF16)
+
+    def ag_start(w, h):
+        for d, hh, n in chains:
+            if hh == h:
+                ag_send(w, d, h, 0, mine_at)
+
+    def ag_mid(w, i, hs=(0, 1)):
+        for d, h, n in chains:
+            if h in hs and i <= n:
+                j = at(d, -i)
+                wait(hid_half(w, j, h), arecv.at[w, d, h, i - 1])
+                if i < n:
+                    ag_send(w, d, h, i, j)
 
     def o_src(xx, j):
         return out.at[j, :, pl.ds(pl.multiple_of(xx * piece, piece), piece)]
@@ -404,54 +405,59 @@
     first_part([5, 6])
     token_wait(7)
     first_part([7])
-    w_start(2, (0, 1))
+    w_start(2, (0,))
     rs_mid(0, 2)
+    w_start(2, (1,))
     w_forward(1, (0, 1))
     rs_mid(0, 3)
     w_ready(1, (0, 1))
     product(1)
     rs_start(1)
-    for w in range(parts):
-        w_start(w, (2,))
-    rs_final(0)
-    ag_start(0)
+    for h in range(2):
+        rs_final(0, h)
+        ag_start(0, h)
     rs_mid(1, 1)
     w_forward(2, (0, 1))
-    rs_mid(1, 2)
     w_ready(2, (0, 1))
     product(2)
     rs_start(2)
+    rs_mid(1, 2)
+    w_start(0, (2,))
     ag_mid(0, 1)
+    rs_mid(2, 1)
+    w_start(1, (2,))
     rs_mid(1, 3)
-    rs_mid(2, 1)
+    w_start(2, (2,))
+    rs_mid(2, 2)
     ag_mid(0, 2)
-    rs_final(1)
-    ag_start(1)
-    rs_mid(2, 2)
+    rs_final(1, 0)
+    rs_final(1, 1)
+    rs_mid(2, 3)
+    ag_start(1, 0)
+    ag_start(1, 1)
     ag_mid(0, 3)
+    w_forward(0, (2,))
+    w_forward(1, (2,))
+    for h in range(2):
+        rs_final(2, h)
+        ag_start(2, h)
+    w_forward(2, (2,))
+    ag_mid(0, 4)
     ag_mid(1, 1)
-    w_forward(0, (2,))
-    rs_mid(2, 3)
-    ag_mid(0, 4)
-    ag_mid(1, 2)
-    w_forward(1, (2,))
-    w_forward(2, (2,))
-    w_ready(0, (2,))
-    rs_final(2)
-    ag_start(2)
-    w_ready(1, (2,))
-    w_ready(2, (2,))
+    for w in range(parts):
+        w_ready(w, (2,))
     finish_rows([mine_at])
     send_rows([mine_at])
-    ag_mid(1, 3)
     ag_mid(2, 1)
+    ag_mid(1, 2)
     finish_rows([at(0, 1), at(1, 1)])
     send_rows([at(0, 1), at(1, 1)])
-    ag_mid(1, 4)
     ag_mid(2, 2)
+    ag_mid(1, 3)
     finish_rows([at(0, 2), at(1, 2)])
     send_rows([at(0, 2), at(1, 2)])
     ag_mid(2, 3)
+    ag_mid(1, 4)
     finish_rows([at(0, 3), at(1, 3)])
     send_rows([at(0, 3), at(1, 3)])
     ag_mid(2, 4)
@@ -490,15 +496,10 @@
     own_home.start()
 
     for m in range(3):
-        for w in range(parts):
-            wait(weights[m].at[pl.ds(0, nxy - 1), :, pl.ds(w * lane, lane)], wsend.at[m, w])
-            wait(wbuf.at[w, m, :, 0], fsend.at[m, w])
-    for w in range(parts):
-        for d, h, n in chains:
-            for i in range(n):
-                wait(land.at[w, d, h, i], rsend.at[w, d, h, i])
-                for p in range(len(cuts)):
-                    wait(hid_cut(w, mine_at, h, p), asend.at[w, d, h, i, p])
+        wait(weights[m].at[pl.ds(0, nxy - 1)], wsend.at[m])
+    wait(wbuf.at[:, :, :, 0], fsend)
+    wait(part.at[:, pl.ds(0, nz - 1)], rsend)
+    wait(hid.at[:, pl.ds(0, nz - 1)], asend)
     for i in (ny - 2, ny - 1):
         t_sent(i)
     wait(back_ref.at[pl.ds(0, nxy - 1)], bsem.at[0])
@@ -509,7 +510,10 @@
         left = jnp.concatenate([home[zh * nzl + zl] for zl in range(nzl)], axis=1)
         got = jnp.dot(left, perm_back[...], preferred_element_type=F32).astype(BF16)
         for seg, b in enumerate(blocks_of(zh)):
-            final_ref[:, b] = got[:, seg * block : (seg + 1) * block]
+            result[:, b] = got[:, seg * block : (seg + 1) * block]
+    leave = pltpu.make_async_copy(result, final_ref, hsem.at[2])
+    leave.start()
+    leave.wait()
 
 
 def relay(pos, cid, token_count, tokens, names, probs, w_gate, w_up, w_down, cap):
@@ -533,7 +537,7 @@
         lambda *refs: relay_kernel(pos, dims, refs),
         out_shape=jax.ShapeDtypeStruct((tok, feats), BF16),
         in_specs=[smem, vmem, vmem, vmem, any_spec, any_spec, any_spec],
-        out_specs=vmem,
+        out_specs=any_spec,
         scratch_shapes=[
             pltpu.VMEM((nz, tok, piece), BF16),
             pltpu.VMEM((8, tok), F32),
@@ -553,19 +557,20 @@
             pltpu.VMEM((parts, nz, rows, wide), BF16),
             pltpu.VMEM((feats // 2, feats // 2), BF16),
             pltpu.VMEM((nz, rows, nx * piece), BF16),
+            pltpu.VMEM((tok, feats), BF16),
             dma((2,)),
             dma((2,)),
             dma((12,)),
+            dma((3,)),
             dma((3, parts)),
-            dma((3, parts)),
-            dma((3, parts)),
+            dma,
             dma((3, parts)),
             dma((ny,)),
             dma((ny,)),
+            dma,
             dma((parts, 2, 2, nz // 2)),
+            dma,
             dma((parts, 2, 2, nz // 2)),
-            dma((parts, 2, 2, nz // 2, 2)),
-            dma((parts, 2, 2, nz // 2, 2)),
             dma((3,)),
             dma((3,)),
         ],

time: 145 us -> 141 us (0.972)
  Pallas kernels: 142 us -> 137 us
    pallas_call x1, Pallas kernels: 142 us -> 137 us  [relay(): pl.pallas_call(lambda *refs: relay_kernel(pos, dims, refs), out_shape=jax...]
where the time goes in v5:
time: 141 us; the launch traced here: 140 us
  Pallas kernels  137 us (97%)
  local copies, waits for them, and re-layouts  1.67 us (1%)
    pallas_call x1, Pallas kernels, relay(): pl.pallas_call(lambda *refs: relay_kernel(pos, dims, refs), out_shape=jax...  137 us

profile of v5, /device:TPU:1, one launch (start us, length us, event | category | flops | bytes accessed | tf_op | source)
XLA Modules:
  0.0 139.7 jit_solution(5358288262210674561)
XLA Ops:
  0.7 137.4 %relay.1 = bf16[128,1024]{1,0:T(8,128)(2,1)} custom-call(s32[1]{0:T(128)S(6)} %copy.9.refs_0_, bf16[128,1024]{1,0:T(8,128)(2,1)} %refs_1_.1, s32[2,128]{1,0:T(2,128)} %bitcast.2, f32[2,128]{1,0:T(2,128)} %bitcast.3, bf16[32,32,384]{2,1,0:T(8,128)(2,1)} %refs_4_.1, bf16[32,32,384]{2,1,0:T(8,128)(2,1)} %refs_5_.1, bf16[32,32,384]{2,1,0:T(8,128)(2,1)} %refs_6_.1), custom_call_target="tpu_custom_call" | custom-call | tf_op jit(solution)/shard_map/relay/pallas_call | solution.py:536
  138.1 1.7 %copy.10 = bf16[128,1024]{1,0:T(8,128)(2,1)} copy(bf16[128,1024]{1,0:T(8,128)(2,1)} %relay.1) | data formatting | bytes 524288

commit v6 on v5

--- a/solution.py
+++ b/solution.py
@@ -146,14 +146,14 @@
 
     def w_start(w, mats):
         def body(k, carry):
-            xx = lax.rem(x + lax.rem(k, nx), nx)
-            yy = lax.rem(y + k // nx, ny)
+            xx = lax.rem(x + lax.rem(k, nx) + 1, nx)
+            yy = lax.rem(y + far_first(k // nx), ny)
             dev = pos.dev(xx, yy, z, c)
             for m in mats:
                 remote(w_src(m, w, yy * nx + xx), w_dst(m, w, x, y, c), wsend.at[m], wrecv.at[m, w], dev).start()
             return carry
 
-        lax.fori_loop(1, nxy, body, 0)
+        lax.fori_loop(0, nxy - 1, body, 0)
         for m in mats:
             pltpu.make_async_copy(w_src(m, w, y * nx + x), w_dst(m, w, x, y, c), loc.at[2 + 3 * w + m]).start()
 
@@ -178,7 +178,7 @@
     count = nx * rows
 
     def dy_of(i):
-        return lax.rem(3 * nz - z - far_first(i), nz)
+        return lax.rem(6 * nz - 3 * (z + far_first(i)), nz)
 
     def dispatch(i):
         yy = lax.rem(y + dy_of(i), ny)
@@ -273,7 +273,7 @@
         return slice((2 * h + m) * half, (2 * h + m + 1) * half)
 
     def first_part(order):
-        js = [lax.rem(z + y + far_first(i), nz) for i in order]
+        js = [lax.rem(3 * (z + far_first(i)) + y, nz) for i in order]
         left = jnp.concatenate([x_in[j] for j in js], axis=0) if len(js) > 1 else x_in[js[0]]
         for m in range(2):
             res = jnp.dot(left, wbuf[0, m].reshape(ny * 2 * depth, nx * lane), preferred_element_type=F32).astype(BF16)
@@ -302,10 +302,10 @@
     chains = [(d, h, far if h == d else far - 1) for h in range(2) for d in range(2)]
     wide = nx * lane
 
-    mine_at = lax.rem(z + y, nz)
+    mine_at = lax.rem(3 * z + y, nz)
 
     def at(d, k):
-        return lax.rem(mine_at + (k if d == 0 else -k) + 2 * nz, nz)
+        return lax.rem(3 * (z + (k if d == 0 else -k)) + y + 2 * nz, nz)
 
     def rs_send(w, d, h, i, src):
         remote(src, land.at[w, d, h, i], rsend, rrecv.at[w, d, h, i], near[d]).start()

time: 141 us -> 133 us (0.943)
  Pallas kernels: 137 us -> 130 us
    pallas_call x1, Pallas kernels: 137 us -> 130 us  [relay(): pl.pallas_call(lambda *refs: relay_kernel(pos, dims, refs), out_shape=jax...]
where the time goes in v6:
time: 133 us
  Pallas kernels  130 us (98%)
  local copies, waits for them, and re-layouts  1.67 us (1%)
    pallas_call x1, Pallas kernels, relay(): pl.pallas_call(lambda *refs: relay_kernel(pos, dims, refs), out_shape=jax...  130 us

profile of v6, /device:TPU:1, one launch (start us, length us, event | category | flops | bytes accessed | tf_op | source)
XLA Modules:
  0.0 132.8 jit_solution(15622634111409335424)
XLA Ops:
  0.7 130.5 %relay.1 = bf16[128,1024]{1,0:T(8,128)(2,1)} custom-call(s32[1]{0:T(128)S(6)} %copy.9.refs_0_, bf16[128,1024]{1,0:T(8,128)(2,1)} %refs_1_.1, s32[2,128]{1,0:T(2,128)} %bitcast.2, f32[2,128]{1,0:T(2,128)} %bitcast.3, bf16[32,32,384]{2,1,0:T(8,128)(2,1)} %refs_4_.1, bf16[32,32,384]{2,1,0:T(8,128)(2,1)} %refs_5_.1, bf16[32,32,384]{2,1,0:T(8,128)(2,1)} %refs_6_.1), custom_call_target="tpu_custom_call" | custom-call | tf_op jit(solution)/shard_map/relay/pallas_call | solution.py:536
  131.2 1.7 %copy.10 = bf16[128,1024]{1,0:T(8,128)(2,1)} copy(bf16[128,1024]{1,0:T(8,128)(2,1)} %relay.1) | data formatting | bytes 524288

commit v7 on v6

--- a/solution.py
+++ b/solution.py
@@ -255,7 +255,8 @@
     w_forward(0, (0, 1))
     t_sent(4)
     t_sent(5)
-    w_start(1, (0, 1))
+    w_start(1, (0,))
+    w_start(1, (1,))
 
     def token_wait(i):
         dy = dy_of(i)
@@ -281,9 +282,9 @@
                 for h in range(2):
                     part[0, j, :, spot(h, m)] = res[i * rows : (i + 1) * rows, h * half : (h + 1) * half]
 
-    def product(w):
+    def product(w, mats):
         wide = nx * lane
-        for m in range(2):
+        for m in mats:
             right = wbuf[w, m].reshape(ny * 2 * depth, wide)
 
             def body(i, carry):
@@ -362,13 +363,16 @@
     def o_src(xx, j):
         return out.at[j, :, pl.ds(pl.multiple_of(xx * piece, piece), piece)]
 
-    def finish_rows(js):
-        res = None
-        for w in range(parts):
-            left = jnp.concatenate([hid[w, j] for j in js], axis=0) if len(js) > 1 else hid[w, js[0]]
-            right = wbuf[w, 2].reshape(ny * 2 * depth, wide)
-            more = lax.dot_general(left, right, (((1,), (1,)), ((), ())), preferred_element_type=F32)
-            res = more if res is None else res + more
+    def down(w, js):
+        left = jnp.concatenate([hid[w, j] for j in js], axis=0) if len(js) > 1 else hid[w, js[0]]
+        right = wbuf[w, 2].reshape(ny * 2 * depth, wide)
+        return lax.dot_general(left, right, (((1,), (1,)), ((), ())), preferred_element_type=F32)
+
+    def early_rows(js):
+        return functools.reduce(jnp.add, [down(w, js) for w in range(parts - 1)])
+
+    def finish_rows(js, early=None):
+        res = (early_rows(js) if early is None else early) + down(parts - 1, js)
         for i, j in enumerate(js):
             out[j] = res[i * rows : (i + 1) * rows].astype(BF16)
 
@@ -410,16 +414,21 @@
     w_start(2, (1,))
     w_forward(1, (0, 1))
     rs_mid(0, 3)
-    w_ready(1, (0, 1))
-    product(1)
+    w_ready(1, (0,))
+    product(1, (0,))
+    w_ready(1, (1,))
+    product(1, (1,))
     rs_start(1)
     for h in range(2):
         rs_final(0, h)
         ag_start(0, h)
+    w_forward(2, (0,))
     rs_mid(1, 1)
-    w_forward(2, (0, 1))
-    w_ready(2, (0, 1))
-    product(2)
+    w_forward(2, (1,))
+    w_ready(2, (0,))
+    product(2, (0,))
+    w_ready(2, (1,))
+    product(2, (1,))
     rs_start(2)
     rs_mid(1, 2)
     w_start(0, (2,))
@@ -456,12 +465,14 @@
     ag_mid(1, 3)
     finish_rows([at(0, 2), at(1, 2)])
     send_rows([at(0, 2), at(1, 2)])
+    early = early_rows([at(0, 3), at(1, 3)])
     ag_mid(2, 3)
     ag_mid(1, 4)
-    finish_rows([at(0, 3), at(1, 3)])
+    finish_rows([at(0, 3), at(1, 3)], early)
     send_rows([at(0, 3), at(1, 3)])
+    early = early_rows([at(0, 4)])
     ag_mid(2, 4)
-    finish_rows([at(0, 4)])
+    finish_rows([at(0, 4)], early)
     send_rows([at(0, 4)])
 
     pltpu.make_async_copy(o_src(x, y), back_ref.at[y * nx + x], bsem.at[2]).wait()

time: 133 us -> 131 us (0.985)
  Pallas kernels: 130 us -> 128 us
    pallas_call x1, Pallas kernels: 130 us -> 128 us  [relay(): pl.pallas_call(lambda *refs: relay_kernel(pos, dims, refs), out_shape=jax...]
where the time goes in v7:
time: 131 us; the launch traced here: 130 us
  Pallas kernels  128 us (98%)
  local copies, waits for them, and re-layouts  1.67 us (1%)
    pallas_call x1, Pallas kernels, relay(): pl.pallas_call(lambda *refs: relay_kernel(pos, dims, refs), out_shape=jax...  128 us

profile of v7, /device:TPU:1, one launch (start us, length us, event | category | flops | bytes accessed | tf_op | source)
XLA Modules:
  0.0 130.3 jit_solution(9877435628740310239)
XLA Ops:
  0.7 127.9 %relay.1 = bf16[128,1024]{1,0:T(8,128)(2,1)} custom-call(s32[1]{0:T(128)S(6)} %copy.9.refs_0_, bf16[128,1024]{1,0:T(8,128)(2,1)} %refs_1_.1, s32[2,128]{1,0:T(2,128)} %bitcast.2, f32[2,128]{1,0:T(2,128)} %bitcast.3, bf16[32,32,384]{2,1,0:T(8,128)(2,1)} %refs_4_.1, bf16[32,32,384]{2,1,0:T(8,128)(2,1)} %refs_5_.1, bf16[32,32,384]{2,1,0:T(8,128)(2,1)} %refs_6_.1), custom_call_target="tpu_custom_call" | custom-call | tf_op jit(solution)/shard_map/relay/pallas_call | solution.py:547
  128.6 1.7 %copy.10 = bf16[128,1024]{1,0:T(8,128)(2,1)} copy(bf16[128,1024]{1,0:T(8,128)(2,1)} %relay.1) | data formatting | bytes 524288
